TPU v7x, 32 devices: a whole 2x2x4 slice. The times are simulated.
32 devices in a mesh: grp: 8 (over y, x, core), tp: 4 (over z).
Axes of the slice: x: 2, y: 2, z: 4, core: 2. Of those that a mesh axis runs over, the one named last changes fastest.
Arguments:
- text_embeds: bfloat16 [16384, 8192], P('grp', 'tp'), may hold values from -6 to 6
- image_embeds: bfloat16 [8192, 8192], P(('grp', 'tp')), may hold values from -6 to 6
- image_offsets: int32 [16, 2], P('grp'), may hold values from 0 to 768, as said below
- image_counts: int32 [16], P('grp'), may hold values from 1 to 2
- seq_lengths: int32 [16], P('grp'), may hold values from 513 to 1024
- norm_gain: bfloat16 [8192], P('tp'), may hold values from 0.25 to 1.75
- key_weight: bfloat16 [8192, 512], P('tp'), may hold values from -0.0625 to 0.0625
- key_bias: bfloat16 [512], replicated, may hold values from -3 to 3
- key_cotangent: bfloat16 [16384, 512], P(('grp', 'tp')), may hold values from -0.017944336 to 0.017944336
Outputs:
- key_states: bfloat16 [16384, 512], P(('grp', 'tp'))
- weight_grad: float32 [8192, 512], P('tp')
- bias_grad: float32 [512], replicated
- gain_grad: float32 [8192], P('tp')
Inputs may be any that keep to these rules, and one draw needn't show every extreme that they name: `image_offsets`: each sequence's first image_counts slots hold increasing starts of non-intersecting runs of 256 rows that end within its used rows; later slots hold 0.
All inputs are finite; a program needn't handle non-finite values.
Results may differ from a plain program's by a relative error of at most 0.0046.
Values may be sent and summed in bfloat16 or wider, within the bound.
A program may use at most 64 MiB of HBM per device.

v0:
```python
import jax
import jax.numpy as jnp
from jax import lax
from jax.sharding import PartitionSpec as P

D = 8192
PATCH_TOK = 256
MAX_IMG = 2
LEN = 1024


def place_images(text_rows, image_rows, offsets, counts, lengths):
    total_rows = text_rows.shape[0]
    row_ids = jnp.arange(total_rows, dtype=jnp.int32)
    seq_ids = row_ids // LEN
    position = row_ids % LEN
    seq_hot = (seq_ids[:, None] == jnp.arange(offsets.shape[0], dtype=jnp.int32)[None, :]).astype(
        jnp.int32
    )
    row_offsets = jnp.sum(seq_hot[:, :, None] * offsets[None, :, :], axis=1)
    row_counts = jnp.sum(seq_hot * counts[None, :], axis=1)
    row_lengths = jnp.sum(seq_hot * lengths[None, :], axis=1)
    slot_ids = jnp.arange(MAX_IMG, dtype=jnp.int32)
    inside = (
        (slot_ids[None, :] < row_counts[:, None])
        & (position[:, None] >= row_offsets)
        & (position[:, None] < row_offsets + PATCH_TOK)
    )
    inside_int = inside.astype(jnp.int32)
    any_inside = jnp.sum(inside_int, axis=1) > 0
    chosen_slot = jnp.sum(inside_int * slot_ids[None, :], axis=1)
    chosen_start = jnp.sum(inside_int * row_offsets, axis=1)
    source = (seq_ids * MAX_IMG + chosen_slot) * PATCH_TOK + position - chosen_start
    source = jnp.where(any_inside, source, 0)
    picked = jnp.take(image_rows, source, axis=0)
    merged = jnp.where(any_inside[:, None], picked, text_rows)
    row_valid = (position < row_lengths).astype(jnp.float32)
    return (merged, row_valid)


def on_device(
    text_embeds,
    image_embeds,
    image_offsets,
    image_counts,
    seq_lengths,
    norm_gain,
    key_weight,
    key_bias,
    key_cotangent,
):
    image_rows = lax.all_to_all(image_embeds, "tp", split_axis=1, concat_axis=0, tiled=True)
    merged, row_valid = place_images(
        text_embeds, image_rows, image_offsets, image_counts, seq_lengths
    )
    merged32 = merged.astype(jnp.float32)
    squares = lax.psum(jnp.sum(merged32 * merged32, axis=1), "tp")
    rstd = lax.rsqrt(squares / D + 1e-06)
    gain32 = norm_gain.astype(jnp.float32)
    normed = (merged32 * rstd[:, None] * gain32[None, :]).astype(jnp.bfloat16)
    own_count = key_cotangent.shape[0]
    projected = lax.psum_scatter(
        jnp.dot(normed, key_weight, preferred_element_type=jnp.float32),
        "tp",
        scatter_dimension=0,
        tiled=True,
    )
    own_valid = lax.dynamic_slice_in_dim(row_valid, lax.axis_index("tp") * own_count, own_count, 0)
    bias32 = key_bias.astype(jnp.float32)
    key_states = ((projected + bias32[None, :]) * own_valid[:, None]).astype(jnp.bfloat16)
    own_grad = (key_cotangent.astype(jnp.float32) * own_valid[:, None]).astype(jnp.bfloat16)
    masked_grad = lax.all_gather(own_grad, "tp", axis=0, tiled=True)
    weight_local = lax.dot_general(
        normed, masked_grad, (((0,), (0,)), ((), ())), preferred_element_type=jnp.float32
    )
    bias_local = jnp.sum(masked_grad.astype(jnp.float32), axis=0)
    grad_normed = lax.dot_general(
        masked_grad, key_weight, (((1,), (1,)), ((), ())), preferred_element_type=jnp.float32
    )
    gain_local = jnp.sum(grad_normed * merged32 * rstd[:, None], axis=0)
    weight_grad, bias_grad, gain_grad = lax.psum((weight_local, bias_local, gain_local), "grp")
    return (key_states, weight_grad, bias_grad, gain_grad)


def solution(mesh):
    placed = (
        P("grp", "tp"),
        P(("grp", "tp"), None),
        P("grp", None),
        P("grp"),
        P("grp"),
        P("tp"),
        P("tp", None),
        P(),
        P(("grp", "tp"), None),
    )
    return jax.shard_map(
        on_device,
        mesh=mesh,
        in_specs=placed,
        out_specs=(P(("grp", "tp"), None), P("tp", None), P(), P("tp")),
        check_vma=False,
    )
```

profile of v0, /device:TPU:1, one launch (start us, length us, event | category | flops | bytes accessed | tf_op | source)
XLA Modules:
  0.0 387.2 jit_solution(4469457351628642822)
XLA Ops:
  7.2 0.0 copy-start
  7.2 0.0 copy-start.2
  7.2 0.0 copy-start.3
  7.2 0.0 copy-start.5
  7.2 4.9 %copy.18 = bf16[32,4,8,2048]{3,2,0,1:T(8,128)(2,1)} copy(bf16[32,4,8,2048]{3,2,1,0:T(8,128)(2,1)} %bitcast.15) | data formatting | bytes 8388608 | tf_op jit(solution)/shard_map/all_to_all | solution.py:52
  12.2 5.4 %all-to-all-start = ((bf16[256,4,2048]{2,0,1:T(8,128)(2,1)}), bf16[256,4,2048]{2,0,1:T(8,128)(2,1)}, u32[]{:S(2)}, u32[]{:S(2)}) async-start(bf16[256,4,2048]{2,0,1:T(8,128)(2,1)} %bitcast.14), calls=%async_computation | async-start | bytes 8388608 | tf_op jit(solution)/shard_map/all_to_all | solution.py:52
  17.6 0.0 copy-done.3
  17.6 0.1 multiply_reduce_fusion
  17.7 0.1 select_reduce_fusion
  17.8 0.1 select_reduce_fusion.2
  18.0 92.4 %all-to-all-done = bf16[256,4,2048]{2,0,1:T(8,128)(2,1)} async-done(((bf16[256,4,2048]{2,0,1:T(8,128)(2,1)}), bf16[256,4,2048]{2,0,1:T(8,128)(2,1)}, u32[]{:S(2)}, u32[]{:S(2)}) %all-to-all-start) | async-done | bytes 4194336 | tf_op jit(solution)/shard_map/all_to_all | solution.py:52
  110.4 19.1 %gather_fusion = bf16[2048,2048]{1,0:T(8,128)(2,1)} fusion(bf16[1024,2048]{1,0:T(8,128)(2,1)} %bitcast.1, s32[2048]{0:T(1024)S(1)} %broadcast_clamp_fusion), kind=kCustom, calls=%fused_computation | custom fusion | bytes 16785408 | tf_op jit(solution)/shard_map/jit(_take)/gather | solution.py:35
  129.5 10.8 %fusion = (f32[2048]{0:T(1024)S(1)}, bf16[2048,2048]{1,0:T(8,128)(2,1)}) fusion(bf16[2048,2048]{1,0:T(8,128)(2,1)} %param.9, bf16[2048,2048]{1,0:T(8,128)(2,1)} %gather_fusion, pred[2048]{0:T(1024)(128)(4,1)S(1)} %get-tuple-element.13, pred[2048]{0:T(1024)(128)(4,1)S(1)} %get-tuple-element.14), kind=kLoop, calls=%fused_computation.4 | loop fusion | flops 20969472 | bytes 25178112 | tf_op jit(solution)/shard_map/reduce_sum | solution.py:57
  140.3 7.9 %psum.28 = f32[2048]{0:T(1024)S(1)} all-reduce(f32[2048]{0:T(1024)S(1)} %get-tuple-element.11), channel_id=1, replica_groups=mesh['grp'=8,'tp'=4] {'tp'}, use_global_device_ids=true, to_apply=%region_6.7 | all-reduce | flops 2048 | bytes 16384 | tf_op jit(solution)/shard_map/psum | solution.py:57
  148.2 0.0 copy-start.4
  148.3 0.0 copy-start.1
  148.3 10.0 %fusion.7 = f32[2048,512]{1,0:T(8,128)} fusion(bf16[2048,512]{1,0:T(8,128)(2,1)S(1)} %copy-done, bf16[2048,2048]{1,0:T(8,128)(2,1)} %get-tuple-element.12, f32[2048]{0:T(1024)S(1)} %convert_element_type.40, f32[2048]{0:T(1024)S(1)} %add_rsqrt_fusion), kind=kOutput, calls=%fused_computation.13 | convolution fusion | flops 4311744512 | bytes 14696448 | tf_op jit(solution)/shard_map/dot_general | solution.py:63
  158.3 0.0 reduce-scatter.2.cloned.1.call-update
  158.3 0.0 all-gather.2.cloned.1.call-start
  158.4 0.1 fusion.22
  158.5 77.7 %reduce-scatter.2.cloned.1.call-done = f32[512,512]{1,0:T(8,128)} async-done(((f32[2048,512]{1,0:T(8,128)}), f32[512,512]{1,0:T(8,128)}) %reduce-scatter.2.cloned.1.call-update) | async-done | bytes 1048592 | tf_op jit(solution)/shard_map/reduce_scatter | solution.py:62
  236.2 2.4 multiply_convert_fusion
  238.6 0.0 all-gather.2.cloned.1.call-update
  238.6 0.2 all-reduce.3.cloned.1.call-start
  238.8 46.2 %all-gather.2.cloned.1.call-done = bf16[2048,512]{1,0:T(8,128)(2,1)} async-done(((bf16[512,512]{1,0:T(8,128)(2,1)}), bf16[2048,512]{1,0:T(8,128)(2,1)}) %all-gather.2.cloned.1.call-update) | async-done | bytes 2097168 | tf_op jit(solution)/shard_map/all_gather | solution.py:72
  285.1 10.9 %fusion.5 = f32[2048,512]{1,0:T(8,128)} fusion(bf16[2048,512]{1,0:T(8,128)(2,1)} %all-gather.2.cloned.1.call-done, bf16[2048,2048]{1,0:T(8,128)(2,1)} %get-tuple-element.12, f32[2048]{0:T(1024)S(1)} %convert_element_type.40, f32[2048]{0:T(1024)S(1)} %add_rsqrt_fusion), kind=kOutput, calls=%fused_computation.12 | convolution fusion | flops 4311744512 | bytes 14696448 | tf_op jit(solution)/shard_map/dot_general | solution.py:73
  295.9 0.0 all-reduce.3.cloned.1.call-update
  296.0 1.9 convert_reduce_fusion
  297.9 7.9 %fusion.4 = f32[2048]{0:T(1024)S(1)} fusion(bf16[2048,2048]{1,0:T(8,128)(2,1)} %get-tuple-element.12, bf16[2048,512]{1,0:T(8,128)(2,1)} %all-gather.2.cloned.1.call-done, bf16[2048,512]{1,0:T(8,128)(2,1)S(1)} %copy-done, f32[2048]{0:T(1024)S(1)} %add_rsqrt_fusion), kind=kOutput, calls=%fused_computation.8 | convolution fusion | flops 4311742464 | bytes 12599296 | tf_op jit(solution)/shard_map/dot_general | solution.py:77
  305.8 22.2 %all-reduce = (f32[512]{0:T(512)}, f32[2048]{0:T(1024)}) all-reduce(f32[512]{0:T(512)S(1)} %convert_reduce_fusion, f32[2048]{0:T(1024)S(1)} %fusion.4), channel_id=1, replica_groups=mesh['grp'=8,'tp'=4] {'grp'}, use_global_device_ids=true, to_apply=%region_11.12 | all-reduce | flops 2560 | bytes 20480 | tf_op jit(solution)/shard_map/psum | solution.py:81
  328.0 48.0 %all-reduce.3.cloned.1.call-done = f32[2048,512]{1,0:T(8,128)} async-done(((f32[2048,512]{1,0:T(8,128)}), f32[2048,512]{1,0:T(8,128)}) %all-reduce.3.cloned.1.call-update) | async-done | bytes 4194320 | tf_op jit(solution)/shard_map/psum | solution.py:81
  376.0 4.6 %copy.20 = f32[2048,512]{1,0:T(8,128)} copy(f32[2048,512]{1,0:T(8,128)} %all-reduce.3.cloned.1.call-done) | data formatting | bytes 8388608
  (17 shorter events, 0.1 us)
Async XLA Ops:
  7.2 141.1 %copy-start = (bf16[2048,512]{1,0:T(8,128)(2,1)S(1)}, bf16[2048,512]{1,0:T(8,128)(2,1)}, u32[]{:S(2)}) copy-start(bf16[2048,512]{1,0:T(8,128)(2,1)} %param.15) | copy-start | bytes 6291460
  7.2 10.4 %copy-start.2 = (bf16[2048]{0:T(1024)(128)(2,1)S(1)}, bf16[2048]{0:T(1024)(128)(2,1)}, u32[]{:S(2)}) copy-start(bf16[2048]{0:T(1024)(128)(2,1)} %param.14) | copy-start | bytes 12292
  7.2 10.4 %copy-start.3 = (s32[2,2]{1,0:T(2,128)S(1)}, s32[2,2]{1,0:T(2,128)}, u32[]{:S(2)}) copy-start(s32[2,2]{1,0:T(2,128)} %param.11) | copy-start | bytes 52
  7.2 10.5 %copy-start.5 = (s32[2]{0:T(128)S(1)}, s32[2]{0:T(128)}, u32[]{:S(2)}) copy-start(s32[2]{0:T(128)} %param.13) | copy-start | bytes 28
  7.2 10.5 %copy-start.6 = (s32[2]{0:T(128)S(1)}, s32[2]{0:T(128)}, u32[]{:S(2)}) copy-start(s32[2]{0:T(128)} %param.12) | copy-start | bytes 28
  12.2 98.3 %all-to-all-start = ((bf16[256,4,2048]{2,0,1:T(8,128)(2,1)}), bf16[256,4,2048]{2,0,1:T(8,128)(2,1)}, u32[]{:S(2)}, u32[]{:S(2)}) async-start(bf16[256,4,2048]{2,0,1:T(8,128)(2,1)} %bitcast.14), calls=%async_computation | async-start | bytes 8388608 | tf_op jit(solution)/shard_map/all_to_all | solution.py:52
  17.6 218.6 %reduce-scatter.2.cloned.1.call-start = ((), (), s32[]{:S(2)}) async-start(), calls=%async_computation.2 | async-start | bytes 5242880 | tf_op jit(solution)/shard_map/reduce_scatter | solution.py:62
  148.2 10.1 %copy-start.4 = (bf16[512]{0:T(512)(128)(2,1)S(1)}, bf16[512]{0:T(512)(128)(2,1)}, u32[]{:S(2)}) copy-start(bf16[512]{0:T(512)(128)(2,1)} %param.16) | copy-start | bytes 3076
  148.3 87.9 %copy-start.1 = (bf16[512,512]{1,0:T(8,128)(2,1)S(1)}, bf16[512,512]{1,0:T(8,128)(2,1)}, u32[]{:S(2)}) copy-start(bf16[512,512]{1,0:T(8,128)(2,1)} %param.17) | copy-start | bytes 1572868
  158.3 126.7 %all-gather.2.cloned.1.call-start = ((), (), s32[]{:S(2)}) async-start(), calls=%async_computation.3 | async-start | bytes 2621440 | tf_op jit(solution)/shard_map/all_gather | solution.py:72
  238.6 137.4 %all-reduce.3.cloned.1.call-start = ((), (), s32[]{:S(2)}) async-start(), calls=%async_computation.4 | async-start | bytes 8388608 | tf_op jit(solution)/shard_map/psum | solution.py:81
Sparse Core Ops, SparseCore 0:
  158.5 77.6 reduce-scatter.1
  238.7 46.2 all-gather.1
  296.1 79.9 all-reduce.2
where the time goes:
time: 388 us; the launch traced here: 387 us
  waiting for transfers between devices  264 us (68%)
  blocking collectives  30.1 us (8%)
  matrix products  28.8 us (7%)
  local copies, waits for them, and re-layouts  28.7 us (7%)
  other arithmetic  15.6 us (4%)
  between operations  13.9 us (4%)
  starting transfers between devices  5.67 us (1%)
    all_to_all x1, waiting for transfers between devices, on_device(): lax.all_to_all(image_embeds, 'tp', split_axis=1, concat_axis=0, tiled=True)  92.4 us
    reduce_scatter x1, waiting for transfers between devices, on_device(): lax.psum_scatter(jnp.dot(normed, key_weight, preferred_element_type=jnp.f...  77.7 us
    psum x1, waiting for transfers between devices, on_device(): lax.psum((weight_local, bias_local, gain_local), 'grp')  48 us
    all_gather x1, waiting for transfers between devices, on_device(): masked_grad = lax.all_gather(own_grad, 'tp', axis=0, tiled=True)  46.2 us
    psum x1, blocking collectives, on_device(): lax.psum((weight_local, bias_local, gain_local), 'grp')  22.2 us
    gather x1, local copies, waits for them, and re-layouts, place_images(): picked = jnp.take(image_rows, source, axis=0)  19.1 us
    dot_general x1, matrix products, on_device(): lax.dot_general(normed, masked_grad, (((0,), (0,)), ((), ())), preferred_...  10.9 us
    reduce_sum x1, other arithmetic, on_device(): squares = lax.psum(jnp.sum(merged32 * merged32, axis=1), 'tp')  10.8 us
  transfers between devices with their start and end apart: 4, of which 4 were waited for; matrix products, arithmetic and copies ran while one was open for 3% of the time, Pallas kernels for 0%

commit v1 on v0

v1 whole, which is shorter than its diff:
```python
import jax
import jax.numpy as jnp
from jax import lax
from jax.sharding import PartitionSpec as P

EPS = 1e-06
F32 = jnp.float32
BF16 = jnp.bfloat16


def on_device(
    text_embeds,
    image_embeds,
    image_offsets,
    image_counts,
    seq_lengths,
    norm_gain,
    key_weight,
    key_bias,
    key_cotangent,
):
    n_tp = lax.axis_size("tp")
    me = lax.axis_index("tp")
    rows = text_embeds.shape[0]
    width = image_embeds.shape[1]
    seqs, slots = image_offsets.shape
    length = rows // seqs
    own_image = image_embeds.shape[0]
    image_total = own_image * n_tp
    patch = image_total // (seqs * slots)
    own_count = key_cotangent.shape[0]

    image_rows = lax.all_to_all(image_embeds, "tp", split_axis=1, concat_axis=0, tiled=True)

    position = lax.broadcasted_iota(jnp.int32, (seqs, length), 1)
    row_valid = (position < seq_lengths[:, None]).astype(F32).reshape(rows)
    own_valid = lax.dynamic_slice_in_dim(row_valid, me * own_count, own_count, 0)
    own_grad = lax.optimization_barrier(
        (key_cotangent.astype(F32) * own_valid[:, None]).astype(BF16)
    )
    masked_grad = lax.all_gather(own_grad, "tp", axis=0, tiled=True)
    bias_grad = lax.psum(jnp.sum(own_grad.astype(F32), axis=0), ("grp", "tp"))

    text32 = text_embeds.astype(F32)
    image32 = image_embeds.astype(F32)
    image_squares = lax.dynamic_update_slice_in_dim(
        jnp.zeros((image_total,), F32), jnp.sum(image32 * image32, axis=1), me * own_image, 0
    )
    squares = lax.psum(
        jnp.concatenate([jnp.sum(text32 * text32, axis=1), image_squares]), "tp"
    )
    rstd = lax.rsqrt(squares / width + EPS)

    slot_used = lax.broadcasted_iota(jnp.int32, (seqs, slots), 1) < image_counts[:, None]
    inside = jnp.zeros((seqs, length), jnp.bool_)
    source = jnp.zeros((seqs, length), jnp.int32)
    first = lax.broadcasted_iota(jnp.int32, (seqs, length), 0) * (slots * patch)
    for k in range(slots):
        start = image_offsets[:, k : k + 1]
        here = slot_used[:, k : k + 1] & (position >= start) & (position < start + patch)
        source = jnp.where(here, first + k * patch + position - start, source)
        inside = inside | here
    text_rstd = rstd[:rows] * (1.0 - inside.astype(F32).reshape(rows))
    image_rstd = rstd[rows:]
    used = jnp.repeat(slot_used.reshape(-1).astype(F32), patch)

    gain32 = norm_gain.astype(F32)
    scaled_weight = (key_weight.astype(F32) * gain32[:, None]).astype(BF16)
    partial = (
        jnp.dot(text_embeds, scaled_weight, preferred_element_type=F32) * text_rstd[:, None]
    ).astype(BF16)
    text_grad = (masked_grad.astype(F32) * text_rstd[:, None]).astype(BF16)
    slot_starts = (
        lax.broadcasted_iota(jnp.int32, (seqs, slots), 0) * length + image_offsets
    ).reshape(-1)
    image_at = (
        slot_starts[:, None] + lax.broadcasted_iota(jnp.int32, (seqs * slots, patch), 1)
    ).reshape(-1)
    picked = jnp.take(masked_grad, image_at, axis=0, mode="clip")
    image_grad = (picked.astype(F32) * (image_rstd * used)[:, None]).astype(BF16)
    over_rows = (((0,), (0,)), ((), ()))
    text_part = lax.dot_general(text_embeds, text_grad, over_rows, preferred_element_type=F32)

    image_keys = (
        jnp.dot(image_rows, scaled_weight, preferred_element_type=F32) * image_rstd[:, None]
    ).astype(BF16)
    placed = jnp.take(image_keys, source.reshape(rows), axis=0, mode="clip")
    partial = jnp.where(inside.reshape(rows)[:, None], placed, partial)
    partial, masked_grad, bias_grad = lax.optimization_barrier((partial, masked_grad, bias_grad))
    projected = lax.psum_scatter(partial, "tp", scatter_dimension=0, tiled=True)
    key_states = (
        (projected.astype(F32) + key_bias.astype(F32)[None, :]) * own_valid[:, None]
    ).astype(BF16)

    image_part = lax.dot_general(image_rows, image_grad, over_rows, preferred_element_type=F32)
    total = lax.psum((text_part + image_part).astype(BF16), "grp").astype(F32)
    weight_grad = total * gain32[:, None]
    gain_grad = jnp.sum(total * key_weight.astype(F32), axis=1)
    return (key_states, weight_grad, bias_grad, gain_grad)


def solution(mesh):
    placed = (
        P("grp", "tp"),
        P(("grp", "tp"), None),
        P("grp", None),
        P("grp"),
        P("grp"),
        P("tp"),
        P("tp", None),
        P(),
        P(("grp", "tp"), None),
    )
    return jax.shard_map(
        on_device,
        mesh=mesh,
        in_specs=placed,
        out_specs=(P(("grp", "tp"), None), P("tp", None), P(), P("tp")),
        check_vma=False,
    )
```

time: 388 us -> 349 us (0.90)
  waiting for transfers between devices: 264 us -> 89.1 us
  blocking collectives: 30.1 us -> 152 us
  local copies, waits for them, and re-layouts: 28.7 us -> 41.5 us
    psum x2, blocking collectives: 30.1 us -> 152 us  [the longest x1 138 us: on_device(): bias_grad = lax.psum(jnp.sum(own_grad.astype(F32), axis=0), ('grp', 'tp'))]
    all_to_all x1, waiting for transfers between devices: 92.4 us -> 0.01 us  [on_device(): lax.all_to_all(image_embeds, 'tp', split_axis=1, concat_axis=0, tiled=True)]
    all_gather x1, waiting for transfers between devices: 46.2 us -> 0.02 us  [on_device(): masked_grad = lax.all_gather(own_grad, 'tp', axis=0, tiled=True)]
    reduce_scatter x1, waiting for transfers between devices: 77.7 us -> 35.5 us  [on_device(): projected = lax.psum_scatter(partial, 'tp', scatter_dimension=0, tiled=True)]
    unnamed x15 -> x47, local copies, waits for them, and re-layouts: 4.68 us -> 16 us
    psum x1, waiting for transfers between devices: 48 us -> 53.5 us  [on_device(): total = lax.psum((text_part + image_part).astype(BF16), 'grp').astype(F32)]
    gather x1 -> x3, local copies, waits for them, and re-layouts: 19.1 us -> 15.1 us  [the longest x2 10 us: on_device(): placed = jnp.take(image_keys, source.reshape(rows), axis=0, mode='clip')]
    dot_general x3 -> x4, matrix products: 28.8 us -> 28.2 us  [the longest x1 9.47 us: on_device(): jnp.dot(text_embeds, scaled_weight, preferred_element_type=F32)]
  transfers between devices with their start and end apart: 4 -> 4, of which waited for: 4 -> 2; matrix products, arithmetic and copies ran while one was open for 3% -> 12% of each run, Pallas kernels for 0% -> 0%
where the time goes in v1:
time: 349 us; the launch traced here: 347 us
  blocking collectives  152 us (44%)
  waiting for transfers between devices  89.1 us (26%)
  local copies, waits for them, and re-layouts  41.5 us (12%)
  matrix products  28.2 us (8%)
  other arithmetic  16.1 us (5%)
  between operations  14 us (4%)
  starting transfers between devices  5.99 us (2%)
    psum x1, blocking collectives, on_device(): bias_grad = lax.psum(jnp.sum(own_grad.astype(F32), axis=0), ('grp', 'tp'))  138 us
    psum x1, waiting for transfers between devices, on_device(): total = lax.psum((text_part + image_part).astype(BF16), 'grp').astype(F32)  53.5 us
    reduce_scatter x1, waiting for transfers between devices, on_device(): projected = lax.psum_scatter(partial, 'tp', scatter_dimension=0, tiled=True)  35.5 us
    unnamed x47, local copies, waits for them, and re-layouts  16 us
    psum x1, blocking collectives, on_device(): lax.psum(jnp.concatenate([jnp.sum(text32 * text32, axis=1), image_squares...  13.9 us
    gather x2, local copies, waits for them, and re-layouts, on_device(): placed = jnp.take(image_keys, source.reshape(rows), axis=0, mode='clip')  10 us
    dot_general x1, matrix products, on_device(): jnp.dot(text_embeds, scaled_weight, preferred_element_type=F32)  9.47 us
    dot_general x1, matrix products, on_device(): lax.dot_general(text_embeds, text_grad, over_rows, preferred_element_type...  9.33 us
  transfers between devices with their start and end apart: 4, of which 2 were waited for; matrix products, arithmetic and copies ran while one was open for 12% of the time, Pallas kernels for 0%

profile of v1, /device:TPU:1, one launch (start us, length us, event | category | flops | bytes accessed | tf_op | source)
XLA Modules:
  0.0 347.2 jit_solution(14095932493099703073)
XLA Ops:
  7.2 6.4 %copy.28 = bf16[256,8192]{0,1:T(8,128)(2,1)} copy(bf16[256,8192]{1,0:T(8,128)(2,1)} %param.10) | data formatting | bytes 8388608 | tf_op args[1]
  13.6 5.7 %all-to-all-start = ((bf16[256,4,2048]{0,2,1:T(8,128)(2,1)}), bf16[256,4,2048]{0,2,1:T(8,128)(2,1)}, u32[]{:S(2)}, u32[]{:S(2)}) async-start(bf16[256,4,2048]{0,2,1:T(8,128)(2,1)} %bitcast.74), calls=%async_computation | async-start | bytes 8388608 | tf_op jit(solution)/shard_map/all_to_all | solution.py:33
  19.3 0.2 copy.32
  19.6 0.9 multiply_convert_fusion.7
  20.7 0.2 slice_reduce_fusion.1
  20.9 0.2 add_reduce_fusion.1
  21.1 0.1 and_or_fusion
  21.6 0.1 reshape.320
  21.9 2.5 copy.27
  24.6 3.1 multiply_reduce_fusion.1
  27.7 0.3 dynamic_update_slice.3
  28.0 0.1 convert_reduce_fusion
  28.1 138.3 %psum.22 = f32[512]{0:T(512)} all-reduce(f32[512]{0:T(512)S(1)} %convert_reduce_fusion), channel_id=1, replica_groups=mesh['grp'=8,'tp'=4] {'grp','tp'}, use_global_device_ids=true, to_apply=%region_4.0 | all-reduce | flops 512 | bytes 4096 | tf_op jit(solution)/shard_map/psum | solution.py:42
  166.4 5.1 %multiply_reduce_fusion = f32[2048]{0:T(1024)S(1)} fusion(bf16[2048,2048]{1,0:T(8,128)(2,1)} %param.9), kind=kLoop, calls=%fused_computation.2 | loop fusion | flops 12580864 | bytes 8396800 | tf_op jit(solution)/shard_map/reduce_sum | solution.py:50
  171.5 13.9 %psum.21 = f32[3072]{0:T(1024)S(1)} all-reduce(f32[3072]{0:T(1024)S(1)} %pad_maximum_fusion), channel_id=1, replica_groups=mesh['grp'=8,'tp'=4] {'tp'}, use_global_device_ids=true, to_apply=%region_2.0 | all-reduce | flops 3072 | bytes 24576 | tf_op jit(solution)/shard_map/psum | solution.py:49
  185.5 2.9 copy.33
  188.4 5.1 %gather_fusion.1 = bf16[1024,512]{1,0:T(8,128)(2,1)} fusion(bf16[2048,512]{1,0:T(8,128)(2,1)S(1)} %copy.33, s32[1024]{0:T(1024)S(1)} %broadcast_clamp_fusion.1), kind=kCustom, calls=%fused_computation.1 | custom fusion | bytes 2101248 | tf_op jit(solution)/shard_map/jit(_take)/gather | solution.py:79
  193.5 6.3 %copy.29 = bf16[4,256,2048]{2,1,0:T(8,128)(2,1)} copy(bf16[4,256,2048]{1,2,0:T(8,128)(2,1)} %bitcast.1) | data formatting | bytes 8388608 | tf_op jit(solution)/shard_map/all_to_all | solution.py:33
  199.8 4.6 %fusion.11 = bf16[1024,512]{0,1:T(8,128)(2,1)S(1)} fusion(bf16[1024,2048]{1,0:T(8,128)(2,1)} %bitcast.72, bf16[2048,512]{0,1:T(8,128)(2,1)S(1)} %copy-done, f32[2048]{0:T(1024)S(1)} %convert_element_type.85, f32[1024]{0:T(1024)S(1)} %get-tuple-element.29), kind=kOutput, calls=%fused_computation.19 | convolution fusion | flops 2151677952 | bytes 7352320 | tf_op jit(solution)/shard_map/dot_general | solution.py:85
  204.4 0.5 copy.30
  204.9 7.5 %gather_fusion = bf16[2048,512]{1,0:T(8,128)(2,1)S(1)} fusion(bf16[1024,512]{1,0:T(8,128)(2,1)S(1)} %copy.30, s32[2048]{0:T(1024)S(1)} %broadcast_clamp_fusion), kind=kCustom, calls=%fused_computation | custom fusion | bytes 4202496 | tf_op jit(solution)/shard_map/jit(_take)/gather | solution.py:87
  212.5 2.5 copy.31
  215.0 4.9 %fusion.14 = f32[512,2048]{1,0:T(8,128)S(1)} fusion(bf16[1024,2048]{1,0:T(8,128)(2,1)} %bitcast.73, bf16[1024,512]{1,0:T(8,128)(2,1)S(1)} %copy-done.2, f32[1024]{0:T(1024)S(1)} %get-tuple-element.28), kind=kOutput, calls=%fused_computation.20 | convolution fusion | flops 2149056512 | bytes 9441280 | tf_op jit(solution)/shard_map/dot_general | solution.py:95
  219.9 9.3 %fusion.3 = bf16[2048,512]{0,1:T(8,128)(2,1)} fusion(f32[512,2048]{1,0:T(8,128)S(1)} %fusion.14, bf16[2048,2048]{1,0:T(8,128)(2,1)} %param.9, bf16[2048,512]{0,1:T(8,128)(2,1)S(1)} %copy-done.5, f32[2048]{0:T(1024)S(1)} %slice_multiply_fusion), kind=kOutput, calls=%fused_computation.13 | convolution fusion | flops 4300210176 | bytes 16785408 | tf_op jit(solution)/shard_map/dot_general | solution.py:82
  229.3 0.3 reduce-scatter.2.cloned.1.call-start
  229.6 9.5 %fusion.4 = bf16[2048,512]{0,1:T(8,128)(2,1)} fusion(bf16[2048,512]{0,1:T(8,128)(2,1)} %copy.31, bf16[2048,2048]{1,0:T(8,128)(2,1)} %param.9, f32[2048]{0:T(1024)S(1)} %slice_multiply_fusion, pred[2048]{0:T(1024)(128)(4,1)S(1)} %or.12, bf16[2048,512]{0,1:T(8,128)(2,1)S(1)} %copy-done.1, f32[2048]{0:T(1024)S(1)} %convert_element_type.85), kind=kOutput, calls=%fused_computation.14 | convolution fusion | flops 4301258752 | bytes 14698496 | tf_op jit(solution)/shard_map/dot_general | solution.py:70
  239.1 53.5 %all-reduce.2.cloned.1.call-done = bf16[2048,512]{0,1:T(8,128)(2,1)} async-done(((bf16[2048,512]{0,1:T(8,128)(2,1)}), bf16[2048,512]{0,1:T(8,128)(2,1)}) %all-reduce.2.cloned.1.call-update) | async-done | bytes 2097168 | tf_op jit(solution)/shard_map/psum | solution.py:96
  292.6 4.9 %fusion.1 = (f32[2048]{0:T(1024)}, f32[2048,512]{0,1:T(8,128)}) fusion(bf16[2048,512]{0,1:T(8,128)(2,1)S(1)} %copy-done.1, bf16[2048,512]{0,1:T(8,128)(2,1)} %all-reduce.2.cloned.1.call-done, f32[2048]{0:T(1024)S(1)} %convert_element_type.85), kind=kLoop, calls=%fused_computation.8 | loop fusion | flops 5240832 | bytes 8404992 | tf_op jit(solution)/shard_map/reduce_sum | solution.py:98
  297.6 5.3 %copy.35 = f32[2048,512]{1,0:T(8,128)} copy(f32[2048,512]{0,1:T(8,128)} %get-tuple-element.27) | data formatting | bytes 8388608
  302.9 35.5 %reduce-scatter.2.cloned.1.call-done = bf16[512,512]{0,1:T(8,128)(2,1)} async-done(((bf16[2048,512]{0,1:T(8,128)(2,1)}), bf16[512,512]{0,1:T(8,128)(2,1)}) %reduce-scatter.2.cloned.1.call-update) | async-done | bytes 524304 | tf_op jit(solution)/shard_map/reduce_scatter | solution.py:90
  338.4 1.2 multiply_convert_fusion.6
  339.7 1.0 copy.34
  (69 shorter events, 1.2 us)
Async XLA Ops:
  13.5 5.7 %copy-start.10 = (s32[2]{0:T(128)S(1)}, s32[2]{0:T(128)}, u32[]{:S(2)}) copy-start(s32[2]{0:T(128)} %param.13) | copy-start | bytes 28
  13.5 5.8 %copy-start.6 = (bf16[512,512]{1,0:T(8,128)(2,1)S(1)}, bf16[512,512]{1,0:T(8,128)(2,1)}, u32[]{:S(2)}) copy-start(bf16[512,512]{1,0:T(8,128)(2,1)} %param.17) | copy-start | bytes 1572868
  13.5 7.1 %copy-start.11 = (s32[2]{0:T(128)S(1)}, s32[2]{0:T(128)}, u32[]{:S(2)}) copy-start(s32[2]{0:T(128)} %param.12) | copy-start | bytes 28
  13.5 7.3 %copy-start.7 = (s32[2,2]{1,0:T(2,128)S(1)}, s32[2,2]{1,0:T(2,128)}, u32[]{:S(2)}) copy-start(s32[2,2]{1,0:T(2,128)} %param.11) | copy-start | bytes 52
  13.5 8.3 %copy-start.4 = (bf16[2048,512]{1,0:T(8,128)(2,1)S(1)}, bf16[2048,512]{1,0:T(8,128)(2,1)}, u32[]{:S(2)}) copy-start(bf16[2048,512]{1,0:T(8,128)(2,1)} %param.15) | copy-start | bytes 6291460
  13.6 179.9 %all-to-all-start = ((bf16[256,4,2048]{0,2,1:T(8,128)(2,1)}), bf16[256,4,2048]{0,2,1:T(8,128)(2,1)}, u32[]{:S(2)}, u32[]{:S(2)}) async-start(bf16[256,4,2048]{0,2,1:T(8,128)(2,1)} %bitcast.74), calls=%async_computation | async-start | bytes 8388608 | tf_op jit(solution)/shard_map/all_to_all | solution.py:33
  19.2 5.2 %copy-start.8 = (bf16[2048]{0:T(1024)(128)(2,1)S(1)}, bf16[2048]{0:T(1024)(128)(2,1)}, u32[]{:S(2)}) copy-start(bf16[2048]{0:T(1024)(128)(2,1)} %param.14) | copy-start | bytes 12292
  19.2 166.3 %all-gather.2.cloned.1.call-start = ((), (), s32[]{:S(2)}) async-start(), calls=%async_computation.2 | async-start | bytes 2621440 | tf_op jit(solution)/shard_map/all_gather | solution.py:41
  20.5 272.1 %all-reduce.2.cloned.1.call-start = ((), (), s32[]{:S(2)}) async-start(), calls=%async_computation.4 | async-start | bytes 4194304 | tf_op jit(solution)/shard_map/psum | solution.py:96
  21.9 6.1 %copy-start.3 = (bf16[512,512]{0,1:T(8,128)(2,1)S(1)}, bf16[512,512]{0,1:T(8,128)(2,1)}, u32[]{:S(2)}) copy-start(bf16[512,512]{0,1:T(8,128)(2,1)} %multiply_convert_fusion.7) | copy-start | bytes 1572868
  193.5 6.4 %copy-start = (bf16[2048,512]{0,1:T(8,128)(2,1)S(1)}, bf16[2048,512]{0,1:T(8,128)(2,1)}, u32[]{:S(2)}) copy-start(bf16[2048,512]{0,1:T(8,128)(2,1)} %copy.27) | copy-start | bytes 6291460
  212.5 2.5 copy-start.2
  215.0 4.9 %copy-start.5 = (bf16[2048,512]{0,1:T(8,128)(2,1)S(1)}, bf16[2048,512]{0,1:T(8,128)(2,1)}, u32[]{:S(2)}) copy-start(bf16[2048,512]{0,1:T(8,128)(2,1)} %all-gather.2.cloned.1.call-done) | copy-start | bytes 6291460
  219.9 9.6 %copy-start.1 = (bf16[2048,512]{0,1:T(8,128)(2,1)S(1)}, bf16[2048,512]{0,1:T(8,128)(2,1)}, u32[]{:S(2)}) copy-start(bf16[2048,512]{0,1:T(8,128)(2,1)} %copy.27) | copy-start | bytes 6291460
  229.3 9.8 %copy-start.9 = (bf16[512]{0:T(512)(128)(2,1)S(1)}, bf16[512]{0:T(512)(128)(2,1)}, u32[]{:S(2)}) copy-start(bf16[512]{0:T(512)(128)(2,1)} %param.16) | copy-start | bytes 3076
  229.3 109.2 %reduce-scatter.2.cloned.1.call-start = ((), (), s32[]{:S(2)}) async-start(), calls=%async_computation.3 | async-start | bytes 2621440 | tf_op jit(solution)/shard_map/reduce_scatter | solution.py:90
Sparse Core Ops, SparseCore 0:
  22.2 77.7 all-gather.1
  229.4 63.1 all-reduce.1
  294.9 43.4 reduce-scatter.1

commit v2 on v1

--- a/solution.py
+++ b/solution.py
@@ -1,11 +1,160 @@
+import functools
+
 import jax
 import jax.numpy as jnp
 from jax import lax
+from jax.experimental import pallas as pl
+from jax.experimental.pallas import tpu as pltpu
 from jax.sharding import PartitionSpec as P
 
 EPS = 1e-06
 F32 = jnp.float32
 BF16 = jnp.bfloat16
+
+
+def reduce_kernel(
+    n_grp,
+    n_tp,
+    keys_ref,
+    weight_ref,
+    bias_ref,
+    keys_out,
+    weight_out,
+    bias_out,
+    keys_buf,
+    weight_buf,
+    bias_buf,
+    chunk_buf,
+    full_buf,
+    keys_send,
+    keys_recv,
+    weight_send,
+    weight_recv,
+    bias_send,
+    bias_recv,
+    full_send,
+    full_recv,
+):
+    g = lax.axis_index("grp")
+    t = lax.axis_index("tp")
+    own = keys_out.shape[0]
+    chunk = chunk_buf.shape[0]
+
+    barrier = pltpu.get_barrier_semaphore()
+    for d in range(1, n_grp):
+        pl.semaphore_signal(barrier, inc=1, device_id={"grp": lax.rem(g + d, n_grp)})
+    for d in range(1, n_tp):
+        pl.semaphore_signal(barrier, inc=1, device_id={"tp": lax.rem(t + d, n_tp)})
+    pl.semaphore_wait(barrier, n_grp + n_tp - 2)
+
+    def rows_of(index, size):
+        return pl.ds(pl.multiple_of(index * size, size), size)
+
+    keys_copies, weight_copies, bias_copies, full_copies = [], [], [], []
+    for d in range(1, n_grp):
+        peer = lax.rem(g + d, n_grp)
+        copy = pltpu.make_async_remote_copy(
+            src_ref=weight_ref.at[rows_of(peer, chunk)],
+            dst_ref=weight_buf.at[d - 1],
+            send_sem=weight_send.at[d - 1],
+            recv_sem=weight_recv.at[d - 1],
+            device_id={"grp": peer},
+        )
+        copy.start()
+        weight_copies.append(copy)
+    for d in range(n_tp - 1, 0, -1):
+        peer = lax.rem(t + d, n_tp)
+        copy = pltpu.make_async_remote_copy(
+            src_ref=keys_ref.at[rows_of(peer, own)],
+            dst_ref=keys_buf.at[d - 1],
+            send_sem=keys_send.at[d - 1],
+            recv_sem=keys_recv.at[d - 1],
+            device_id={"tp": peer},
+        )
+        copy.start()
+        keys_copies.append(copy)
+    for d in range(1, n_grp):
+        copy = pltpu.make_async_remote_copy(
+            src_ref=bias_ref,
+            dst_ref=bias_buf.at[d - 1],
+            send_sem=bias_send.at[d - 1],
+            recv_sem=bias_recv.at[d - 1],
+            device_id={"grp": lax.rem(g + d, n_grp)},
+        )
+        copy.start()
+        bias_copies.append(copy)
+
+    for copy in weight_copies:
+        copy.wait()
+    total = weight_ref[rows_of(g, chunk)].astype(F32)
+    for d in range(n_grp - 1):
+        total = total + weight_buf[d].astype(F32)
+    chunk_buf[...] = total.astype(BF16)
+    for d in range(1, n_grp):
+        copy = pltpu.make_async_remote_copy(
+            src_ref=chunk_buf,
+            dst_ref=full_buf.at[g],
+            send_sem=full_send.at[d - 1],
+            recv_sem=full_recv.at[d - 1],
+            device_id={"grp": lax.rem(g + d, n_grp)},
+        )
+        copy.start()
+        full_copies.append(copy)
+    full_buf[g] = chunk_buf[...]
+
+    for copy in bias_copies:
+        copy.wait()
+    total = bias_ref[...]
+    for d in range(n_grp - 1):
+        total = total + bias_buf[d]
+    bias_out[...] = total
+
+    for copy in keys_copies:
+        copy.wait()
+    total = keys_ref[rows_of(t, own)].astype(F32)
+    for d in range(n_tp - 1):
+        total = total + keys_buf[d].astype(F32)
+    keys_out[...] = total
+
+    for copy in full_copies:
+        copy.wait()
+    weight_out[...] = full_buf[...].reshape(weight_out.shape)
+
+
+def reduce_all(n_grp, n_tp, keys, weight, bias):
+    own = keys.shape[0] // n_tp
+    chunk = weight.shape[0] // n_grp
+    columns = keys.shape[1]
+    vmem = pl.BlockSpec(memory_space=pltpu.VMEM)
+    dma = pltpu.SemaphoreType.DMA
+    return pl.pallas_call(
+        functools.partial(reduce_kernel, n_grp, n_tp),
+        out_shape=(
+            jax.ShapeDtypeStruct((own, columns), F32),
+            jax.ShapeDtypeStruct(weight.shape, BF16),
+            jax.ShapeDtypeStruct(bias.shape, F32),
+        ),
+        in_specs=[vmem] * 3,
+        out_specs=(vmem,) * 3,
+        scratch_shapes=[
+            pltpu.VMEM((n_tp - 1, own, columns), BF16),
+            pltpu.VMEM((n_grp - 1, chunk, columns), BF16),
+            pltpu.VMEM((n_grp - 1,) + bias.shape, F32),
+            pltpu.VMEM((chunk, columns), BF16),
+            pltpu.VMEM((n_grp, chunk, columns), BF16),
+            dma((n_tp - 1,)),
+            dma((n_tp - 1,)),
+            dma((n_grp - 1,)),
+            dma((n_grp - 1,)),
+            dma((n_grp - 1,)),
+            dma((n_grp - 1,)),
+            dma((n_grp - 1,)),
+            dma((n_grp - 1,)),
+        ],
+        compiler_params=pltpu.CompilerParams(
+            collective_id=0, has_side_effects=True, vmem_limit_bytes=32 * 1024 * 1024
+        ),
+    )(keys, weight, bias)
 
 
 def on_device(
@@ -30,8 +179,6 @@
     patch = image_total // (seqs * slots)
     own_count = key_cotangent.shape[0]
 
-    image_rows = lax.all_to_all(image_embeds, "tp", split_axis=1, concat_axis=0, tiled=True)
-
     position = lax.broadcasted_iota(jnp.int32, (seqs, length), 1)
     row_valid = (position < seq_lengths[:, None]).astype(F32).reshape(rows)
     own_valid = lax.dynamic_slice_in_dim(row_valid, me * own_count, own_count, 0)
@@ -39,7 +186,6 @@
         (key_cotangent.astype(F32) * own_valid[:, None]).astype(BF16)
     )
     masked_grad = lax.all_gather(own_grad, "tp", axis=0, tiled=True)
-    bias_grad = lax.psum(jnp.sum(own_grad.astype(F32), axis=0), ("grp", "tp"))
 
     text32 = text_embeds.astype(F32)
     image32 = image_embeds.astype(F32)
@@ -49,6 +195,10 @@
     squares = lax.psum(
         jnp.concatenate([jnp.sum(text32 * text32, axis=1), image_squares]), "tp"
     )
+    squares, image_embeds = lax.optimization_barrier((squares, image_embeds))
+    blocks = image_embeds.reshape(own_image, n_tp, -1).transpose(1, 0, 2)
+    image_rows = lax.all_to_all(blocks, "tp", split_axis=0, concat_axis=0, tiled=True)
+    image_rows = image_rows.reshape(image_total, -1)
     rstd = lax.rsqrt(squares / width + EPS)
 
     slot_used = lax.broadcasted_iota(jnp.int32, (seqs, slots), 1) < image_counts[:, None]
@@ -81,19 +231,29 @@
     over_rows = (((0,), (0,)), ((), ()))
     text_part = lax.dot_general(text_embeds, text_grad, over_rows, preferred_element_type=F32)
 
+    image_rows, partial, text_part, image_grad = lax.optimization_barrier(
+        (image_rows, partial, text_part, image_grad)
+    )
     image_keys = (
         jnp.dot(image_rows, scaled_weight, preferred_element_type=F32) * image_rstd[:, None]
     ).astype(BF16)
     placed = jnp.take(image_keys, source.reshape(rows), axis=0, mode="clip")
     partial = jnp.where(inside.reshape(rows)[:, None], placed, partial)
-    partial, masked_grad, bias_grad = lax.optimization_barrier((partial, masked_grad, bias_grad))
-    projected = lax.psum_scatter(partial, "tp", scatter_dimension=0, tiled=True)
+    image_part = lax.dot_general(image_rows, image_grad, over_rows, preferred_element_type=F32)
+    weight_part = (text_part + image_part).astype(BF16)
+    bias_part = jnp.sum(masked_grad.astype(F32).reshape(rows // 8, 8, -1), axis=0)
+    n_grp = lax.axis_size("grp")
+    if weight_part.shape[0] % (n_grp * 16) == 0 and own_count % 16 == 0:
+        projected, total, bias_sum = reduce_all(n_grp, n_tp, partial, weight_part, bias_part)
+    else:
+        projected = lax.psum_scatter(partial, "tp", scatter_dimension=0, tiled=True)
+        total = lax.psum(weight_part, "grp")
+        bias_sum = lax.psum(bias_part, "grp")
     key_states = (
         (projected.astype(F32) + key_bias.astype(F32)[None, :]) * own_valid[:, None]
     ).astype(BF16)
-
-    image_part = lax.dot_general(image_rows, image_grad, over_rows, preferred_element_type=F32)
-    total = lax.psum((text_part + image_part).astype(BF16), "grp").astype(F32)
+    bias_grad = jnp.sum(bias_sum, axis=0)
+    total = total.astype(F32)
     weight_grad = total * gain32[:, None]
     gain_grad = jnp.sum(total * key_weight.astype(F32), axis=1)
     return (key_states, weight_grad, bias_grad, gain_grad)

time: 349 us -> 241 us (0.69)
  blocking collectives: 152 us -> 17.3 us
  Pallas kernels: 0 us -> 51.7 us
  waiting for transfers between devices: 89.1 us -> 69.7 us
  local copies, waits for them, and re-layouts: 41.5 us -> 30.6 us
  other arithmetic: 16.1 us -> 22.6 us
    psum x1 -> x0, blocking collectives: 138 us -> none  [on_device(): bias_grad = lax.psum(jnp.sum(own_grad.astype(F32), axis=0), ('grp', 'tp'))]
    psum x1 -> x0, waiting for transfers between devices: 53.5 us -> none  [on_device(): total = lax.psum((text_part + image_part).astype(BF16), 'grp').astype(F32)]
    pallas_call x0 -> x1, Pallas kernels: none -> 51.7 us  [reduce_all(): pl.pallas_call(functools.partial(reduce_kernel, n_grp, n_tp), out_shape=(...]
    all_to_all x1, waiting for transfers between devices: 0.01 us -> 44.7 us  [on_device(): lax.all_to_all(blocks, 'tp', split_axis=0, concat_axis=0, tiled=True)]
    reduce_scatter x1 -> x0, waiting for transfers between devices: 35.5 us -> none  [on_device(): projected = lax.psum_scatter(partial, 'tp', scatter_dimension=0, tiled=True)]
    all_gather x1, waiting for transfers between devices: 0.02 us -> 25 us  [on_device(): masked_grad = lax.all_gather(own_grad, 'tp', axis=0, tiled=True)]
    unnamed x47 -> x40, local copies, waits for them, and re-layouts: 16 us -> 2.11 us
    optimization_barrier x0 -> x1, local copies, waits for them, and re-layouts: none -> 6.37 us  [on_device(): squares, image_embeds = lax.optimization_barrier((squares, image_embeds))]
  transfers between devices with their start and end apart: 4 -> 2, of which waited for: 2 -> 2; matrix products, arithmetic and copies ran while one was open for 12% -> 19% of each run, Pallas kernels for 0% -> 0%
where the time goes in v2:
time: 241 us; the launch traced here: 240 us
  waiting for transfers between devices  69.7 us (29%)
  Pallas kernels  51.7 us (21%)
  local copies, waits for them, and re-layouts  30.6 us (13%)
  matrix products  28.8 us (12%)
  other arithmetic  22.6 us (9%)
  blocking collectives  17.3 us (7%)
  between operations  14.3 us (6%)
  starting transfers between devices  5.24 us (2%)
    pallas_call x1, Pallas kernels, reduce_all(): pl.pallas_call(functools.partial(reduce_kernel, n_grp, n_tp), out_shape=(...  51.7 us
    all_to_all x1, waiting for transfers between devices, on_device(): lax.all_to_all(blocks, 'tp', split_axis=0, concat_axis=0, tiled=True)  44.7 us
    all_gather x1, waiting for transfers between devices, on_device(): masked_grad = lax.all_gather(own_grad, 'tp', axis=0, tiled=True)  25 us
    psum x1, blocking collectives, on_device(): lax.psum(jnp.concatenate([jnp.sum(text32 * text32, axis=1), image_squares...  17.3 us
    dot_general x1, matrix products, on_device(): lax.dot_general(text_embeds, text_grad, over_rows, preferred_element_type...  12.3 us
    dot_general x1, matrix products, on_device(): jnp.dot(text_embeds, scaled_weight, preferred_element_type=F32)  9.39 us
    gather x1, local copies, waits for them, and re-layouts, on_device(): placed = jnp.take(image_keys, source.reshape(rows), axis=0, mode='clip')  9.21 us
    optimization_barrier x1, local copies, waits for them, and re-layouts, on_device(): squares, image_embeds = lax.optimization_barrier((squares, image_embeds))  6.37 us
  transfers between devices with their start and end apart: 2, of which 2 were waited for; matrix products, arithmetic and copies ran while one was open for 19% of the time, Pallas kernels for 0%

profile of v2, /device:TPU:1, one launch (start us, length us, event | category | flops | bytes accessed | tf_op | source)
XLA Modules:
  0.0 240.2 jit_solution(658754345407618065)
XLA Ops:
  7.2 0.7 fusion.9
  7.9 0.1 dynamic_slice.3
  8.0 2.0 multiply_convert_fusion.4
  10.0 3.1 %multiply_reduce_fusion.1 = f32[256]{0:T(256)S(1)} fusion(bf16[256,8192]{1,0:T(8,128)(2,1)} %param.10), kind=kLoop, calls=%fused_computation.3 | loop fusion | flops 6291200 | bytes 4195328 | tf_op jit(solution)/shard_map/reduce_sum | solution.py:193
  13.2 5.1 %multiply_reduce_fusion = f32[2048]{0:T(1024)S(1)} fusion(bf16[2048,2048]{1,0:T(8,128)(2,1)} %param.9), kind=kLoop, calls=%fused_computation.2 | loop fusion | flops 12580864 | bytes 8396800 | tf_op jit(solution)/shard_map/reduce_sum | solution.py:196
  18.2 0.3 dynamic_update_slice.3
  18.5 17.3 %psum.7 = f32[3072]{0:T(1024)S(1)} all-reduce(f32[3072]{0:T(1024)S(1)} %pad_maximum_fusion), channel_id=1, replica_groups=mesh['grp'=8,'tp'=4] {'tp'}, use_global_device_ids=true, to_apply=%region_2.0 | all-reduce | flops 3072 | bytes 24576 | tf_op jit(solution)/shard_map/psum | solution.py:195
  35.8 6.4 %copy.17 = bf16[256,8192]{0,1:T(8,128)(2,1)} copy(bf16[256,8192]{1,0:T(8,128)(2,1)} %param.10) | data formatting | bytes 8388608 | tf_op jit(solution)/shard_map/optimization_barrier | solution.py:198
  42.2 5.2 %all-to-all-start = ((bf16[4,256,2048]{1,2,0:T(8,128)(2,1)}), bf16[4,256,2048]{1,2,0:T(8,128)(2,1)}, u32[]{:S(2)}, u32[]{:S(2)}) async-start(bf16[4,256,2048]{1,2,0:T(8,128)(2,1)} %bitcast.74), calls=%async_computation | async-start | bytes 8388608 | tf_op jit(solution)/shard_map/all_to_all | solution.py:200
  47.5 0.1 reshape.329
  47.8 0.1 add.88
  48.2 0.2 slice_reduce_fusion.1
  48.3 0.2 slice_reduce_fusion.3
  48.5 0.1 broadcast_bitcast_fusion.1
  49.0 9.4 %fusion.4 = bf16[2048,512]{1,0:T(8,128)(2,1)} fusion(bf16[2048,2048]{1,0:T(8,128)(2,1)} %param.9, f32[2048]{0:T(1024)S(1)} %slice_multiply_fusion, bf16[2048,512]{1,0:T(8,128)(2,1)S(1)} %copy-done.3, f32[2048]{0:T(1024)S(1)} %convert_element_type.76), kind=kOutput, calls=%fused_computation.16 | convolution fusion | flops 4300210176 | bytes 12599296 | tf_op jit(solution)/shard_map/dot_general | solution.py:220
  58.4 25.0 %all-gather.2.cloned.1.call-done = bf16[2048,512]{1,0:T(8,128)(2,1)} async-done(((bf16[512,512]{1,0:T(8,128)(2,1)}), bf16[2048,512]{1,0:T(8,128)(2,1)}) %all-gather.2.cloned.1.call-update) | async-done | bytes 2097168 | tf_op jit(solution)/shard_map/all_gather | solution.py:188
  83.4 6.0 %gather_fusion = bf16[1024,512]{1,0:T(8,128)(2,1)S(1)} fusion(bf16[2048,512]{1,0:T(8,128)(2,1)} %all-gather.2.cloned.1.call-done, s32[1024]{0:T(1024)S(1)} %broadcast_clamp_fusion.1), kind=kCustom, calls=%fused_computation | custom fusion | bytes 2101248 | tf_op jit(solution)/shard_map/jit(_take)/gather | solution.py:229
  89.4 0.3 fusion.2.bias_ref
  89.8 1.3 multiply_convert_fusion.2
  91.0 12.3 %convolution_bitcast_fusion = f32[2048,512]{1,0:T(8,128)} fusion(bf16[2048,2048]{1,0:T(8,128)(2,1)} %param.9, bf16[2048,512]{1,0:T(8,128)(2,1)S(1)} %copy-done.1, f32[2048]{0:T(1024)S(1)} %slice_multiply_fusion), kind=kOutput, calls=%fused_computation.15 | convolution fusion | flops 4298113024 | bytes 14688256 | tf_op jit(solution)/shard_map/dot_general | solution.py:232
  103.3 44.7 %all-to-all-done = bf16[4,256,2048]{1,2,0:T(8,128)(2,1)} async-done(((bf16[4,256,2048]{1,2,0:T(8,128)(2,1)}), bf16[4,256,2048]{1,2,0:T(8,128)(2,1)}, u32[]{:S(2)}, u32[]{:S(2)}) %all-to-all-start) | async-done | bytes 4194336 | tf_op jit(solution)/shard_map/all_to_all | solution.py:200
  148.0 6.2 %copy.18 = bf16[4,256,2048]{2,1,0:T(8,128)(2,1)} copy(bf16[4,256,2048]{1,2,0:T(8,128)(2,1)} %all-to-all-done) | data formatting | bytes 8388608 | tf_op jit(solution)/shard_map/all_to_all | solution.py:200
  154.2 4.7 %multiply_convert_fusion.1 = bf16[1024,512]{1,0:T(8,128)(2,1)S(1)} fusion(bf16[1024,2048]{1,0:T(8,128)(2,1)} %bitcast.75, f32[1024]{0:T(1024)S(1)} %get-tuple-element.30, bf16[2048,512]{1,0:T(8,128)(2,1)S(1)} %copy-done.4, f32[2048]{0:T(1024)S(1)} %convert_element_type.76), kind=kOutput, calls=%fused_computation.17 | convolution fusion | flops 2151677952 | bytes 7352320 | tf_op jit(solution)/shard_map/dot_general | solution.py:238
  159.0 0.3 copy-done.10
  159.2 2.4 add_convert_fusion.weight_ref
  161.6 9.2 %gather_fusion.1 = bf16[2048,512]{1,0:T(8,128)(2,1)} fusion(bf16[1024,512]{1,0:T(8,128)(2,1)S(1)} %multiply_convert_fusion.1, s32[2048]{0:T(1024)S(1)} %broadcast_clamp_fusion), kind=kCustom, calls=%fused_computation.1 | custom fusion | bytes 4202496 | tf_op jit(solution)/shard_map/jit(_take)/gather | solution.py:240
  170.8 2.4 broadcast_select_fusion.keys_ref
  173.2 51.7 %shard_map.120 = (f32[512,512]{1,0:T(8,128)S(1)}, bf16[2048,512]{1,0:T(8,128)(2,1)S(1)}, f32[8,512]{1,0:T(8,128)S(1)}) custom-call(bf16[2048,512]{1,0:T(8,128)(2,1)S(1)} %broadcast_select_fusion.keys_ref, bf16[2048,512]{1,0:T(8,128)(2,1)S(1)} %add_convert_fusion.weight_ref, f32[8,512]{1,0:T(8,128)S(1)} %fusion.2.bias_ref), custom_call_target="tpu_custom_call" | custom-call | tf_op jit(solution)/shard_map/pallas_call | solution.py:130
  224.9 1.3 copy-done
  226.3 0.6 reduce_sum.48
  226.8 5.6 %fusion.3 = (f32[2048]{0:T(1024)}, f32[2048,512]{1,0:T(8,128)}) fusion(bf16[2048,512]{1,0:T(8,128)(2,1)} %param.15, bf16[2048,512]{1,0:T(8,128)(2,1)} %copy-done, f32[2048]{0:T(1024)S(1)} %convert_element_type.76), kind=kLoop, calls=%fused_computation.12 | loop fusion | flops 5240832 | bytes 8404992 | tf_op jit(solution)/shard_map/reduce_sum | solution.py:258
  232.4 0.9 multiply_convert_fusion.3
  (57 shorter events, 0.9 us)
Async XLA Ops:
  7.2 76.3 %all-gather.2.cloned.1.call-start = ((), (), s32[]{:S(2)}) async-start(), calls=%async_computation.1 | async-start | bytes 2621440 | tf_op jit(solution)/shard_map/all_gather | solution.py:188
  42.2 5.2 %copy-start.9 = (s32[2]{0:T(128)S(1)}, s32[2]{0:T(128)}, u32[]{:S(2)}) copy-start(s32[2]{0:T(128)} %param.12) | copy-start | bytes 28
  42.2 5.5 %copy-start.6 = (s32[2,2]{1,0:T(2,128)S(1)}, s32[2,2]{1,0:T(2,128)}, u32[]{:S(2)}) copy-start(s32[2,2]{1,0:T(2,128)} %param.11) | copy-start | bytes 52
  42.2 5.6 %copy-start.8 = (bf16[512]{0:T(512)(128)(2,1)S(1)}, bf16[512]{0:T(512)(128)(2,1)}, u32[]{:S(2)}) copy-start(bf16[512]{0:T(512)(128)(2,1)} %param.16) | copy-start | bytes 3076
  42.2 5.9 %copy-start.7 = (bf16[2048]{0:T(1024)(128)(2,1)S(1)}, bf16[2048]{0:T(1024)(128)(2,1)}, u32[]{:S(2)}) copy-start(bf16[2048]{0:T(1024)(128)(2,1)} %param.14) | copy-start | bytes 12292
  42.2 6.8 %copy-start.3 = (bf16[2048,512]{1,0:T(8,128)(2,1)S(1)}, bf16[2048,512]{1,0:T(8,128)(2,1)}, u32[]{:S(2)}) copy-start(bf16[2048,512]{1,0:T(8,128)(2,1)} %param.15) | copy-start | bytes 6291460
  42.2 105.8 %all-to-all-start = ((bf16[4,256,2048]{1,2,0:T(8,128)(2,1)}), bf16[4,256,2048]{1,2,0:T(8,128)(2,1)}, u32[]{:S(2)}, u32[]{:S(2)}) async-start(bf16[4,256,2048]{1,2,0:T(8,128)(2,1)} %bitcast.74), calls=%async_computation | async-start | bytes 8388608 | tf_op jit(solution)/shard_map/all_to_all | solution.py:200
  83.4 6.0 %copy-start.1 = (bf16[2048,512]{1,0:T(8,128)(2,1)S(1)}, bf16[2048,512]{1,0:T(8,128)(2,1)}, u32[]{:S(2)}) copy-start(bf16[2048,512]{1,0:T(8,128)(2,1)} %all-gather.2.cloned.1.call-done) | copy-start | bytes 6291460
  103.3 50.9 %copy-start.4 = (bf16[2048,512]{1,0:T(8,128)(2,1)S(1)}, bf16[2048,512]{1,0:T(8,128)(2,1)}, u32[]{:S(2)}) copy-start(bf16[2048,512]{1,0:T(8,128)(2,1)} %param.15) | copy-start | bytes 6291460
  154.2 4.8 %copy-start.2 = (bf16[4,256,2048]{2,1,0:T(8,128)(2,1)S(1)}, bf16[4,256,2048]{2,1,0:T(8,128)(2,1)}, u32[]{:S(2)}) copy-start(bf16[4,256,2048]{2,1,0:T(8,128)(2,1)} %copy.18) | copy-start | bytes 12582916
  154.2 4.8 %copy-start.5 = (bf16[1024,512]{1,0:T(8,128)(2,1)S(1)}, bf16[1024,512]{1,0:T(8,128)(2,1)}, u32[]{:S(2)}) copy-start(bf16[1024,512]{1,0:T(8,128)(2,1)} %multiply_convert_fusion.2) | copy-start | bytes 3145732
  154.2 5.0 %copy-start.10 = (f32[2048,512]{1,0:T(8,128)S(1)}, f32[2048,512]{1,0:T(8,128)}, u32[]{:S(2)}) copy-start(f32[2048,512]{1,0:T(8,128)} %convolution_bitcast_fusion) | copy-start | bytes 12582916
  224.9 1.4 copy-start
Sparse Core Ops, SparseCore 0:
  10.2 73.2 all-gather.1

commit v3 on v2

--- a/solution.py
+++ b/solution.py
@@ -5,6 +5,7 @@
 from jax import lax
 from jax.experimental import pallas as pl
 from jax.experimental.pallas import tpu as pltpu
+from jax.experimental.layout import Layout, with_layout_constraint
 from jax.sharding import PartitionSpec as P
 
 EPS = 1e-06
@@ -185,20 +186,29 @@
     own_grad = lax.optimization_barrier(
         (key_cotangent.astype(F32) * own_valid[:, None]).astype(BF16)
     )
-    masked_grad = lax.all_gather(own_grad, "tp", axis=0, tiled=True)
 
     text32 = text_embeds.astype(F32)
     image32 = image_embeds.astype(F32)
-    image_squares = lax.dynamic_update_slice_in_dim(
-        jnp.zeros((image_total,), F32), jnp.sum(image32 * image32, axis=1), me * own_image, 0
-    )
-    squares = lax.psum(
-        jnp.concatenate([jnp.sum(text32 * text32, axis=1), image_squares]), "tp"
-    )
-    squares, image_embeds = lax.optimization_barrier((squares, image_embeds))
-    blocks = image_embeds.reshape(own_image, n_tp, -1).transpose(1, 0, 2)
-    image_rows = lax.all_to_all(blocks, "tp", split_axis=0, concat_axis=0, tiled=True)
-    image_rows = image_rows.reshape(image_total, -1)
+    own_squares = jnp.concatenate(
+        [jnp.sum(text32 * text32, axis=1), jnp.sum(image32 * image32, axis=1)]
+    )
+    high = lax.reduce_precision(own_squares, 8, 7)
+    rest = own_squares - high
+    middle = lax.reduce_precision(rest, 8, 7)
+    terms = jnp.concatenate([high, middle, rest - middle]).astype(BF16)
+    columns = own_grad.shape[1]
+    count = own_squares.shape[0]
+    extra = -(-3 * count // (16 * columns)) * 16
+    terms = jnp.pad(terms, (0, extra * columns - 3 * count)).reshape(extra, columns)
+    gathered = lax.all_gather(jnp.concatenate([own_grad, terms], axis=0), "tp")
+    masked_grad = gathered[:, :own_count].reshape(rows, columns)
+    terms = gathered[:, own_count:].reshape(n_tp, extra * columns)[:, : 3 * count]
+    parts = jnp.sum(terms.astype(F32).reshape(n_tp, 3, count), axis=1)
+    squares = jnp.concatenate(
+        [jnp.sum(parts[:, :rows], axis=0), parts[:, rows:].reshape(image_total)]
+    )
+    image_rows = lax.all_to_all(image_embeds, "tp", split_axis=1, concat_axis=0, tiled=True)
+    image_rows = with_layout_constraint(image_rows, Layout((0, 1)))
     rstd = lax.rsqrt(squares / width + EPS)
 
     slot_used = lax.broadcasted_iota(jnp.int32, (seqs, slots), 1) < image_counts[:, None]
@@ -231,14 +241,18 @@
     over_rows = (((0,), (0,)), ((), ()))
     text_part = lax.dot_general(text_embeds, text_grad, over_rows, preferred_element_type=F32)
 
-    image_rows, partial, text_part, image_grad = lax.optimization_barrier(
-        (image_rows, partial, text_part, image_grad)
+    chosen = jnp.where(inside, source, -1).reshape(rows)
+    place = (
+        chosen[:, None] == lax.broadcasted_iota(jnp.int32, (rows, image_total), 1)
+    ).astype(BF16)
+    image_rows, partial, text_part, image_grad, place = lax.optimization_barrier(
+        (image_rows, partial, text_part, image_grad, place)
     )
     image_keys = (
         jnp.dot(image_rows, scaled_weight, preferred_element_type=F32) * image_rstd[:, None]
     ).astype(BF16)
-    placed = jnp.take(image_keys, source.reshape(rows), axis=0, mode="clip")
-    partial = jnp.where(inside.reshape(rows)[:, None], placed, partial)
+    placed = jnp.dot(place, image_keys, preferred_element_type=F32)
+    partial = (partial.astype(F32) + placed).astype(BF16)
     image_part = lax.dot_general(image_rows, image_grad, over_rows, preferred_element_type=F32)
     weight_part = (text_part + image_part).astype(BF16)
     bias_part = jnp.sum(masked_grad.astype(F32).reshape(rows // 8, 8, -1), axis=0)

time: 241 us -> 237 us (0.983)
  waiting for transfers between devices: 69.7 us -> 97.4 us
  blocking collectives: 17.3 us -> 0 us
  local copies, waits for them, and re-layouts: 30.6 us -> 14 us
  matrix products: 28.8 us -> 35.3 us
  other arithmetic: 22.6 us -> 19.2 us
    all_gather x1, waiting for transfers between devices: 25 us -> 73.9 us  [on_device(): gathered = lax.all_gather(jnp.concatenate([own_grad, terms], axis=0), 'tp')]
    all_to_all x1, waiting for transfers between devices: 44.7 us -> 23.4 us  [on_device(): lax.all_to_all(image_embeds, 'tp', split_axis=1, concat_axis=0, tiled=True)]
    psum x1 -> x0, blocking collectives: 17.3 us -> none  [on_device(): lax.psum(jnp.concatenate([jnp.sum(text32 * text32, axis=1), image_squares...]
    gather x1 -> x0, local copies, waits for them, and re-layouts: 9.21 us -> none  [on_device(): placed = jnp.take(image_keys, source.reshape(rows), axis=0, mode='clip')]
    optimization_barrier x1 -> x0, local copies, waits for them, and re-layouts: 6.37 us -> none  [on_device(): squares, image_embeds = lax.optimization_barrier((squares, image_embeds))]
    dot_general x1, matrix products: 4.74 us -> 10.6 us  [on_device(): placed = jnp.dot(place, image_keys, preferred_element_type=F32)]
    dot_general x1, matrix products: 2.39 us -> 5.88 us  [on_device(): lax.dot_general(image_rows, image_grad, over_rows, preferred_element_type...]
    dot_general x1, matrix products: 9.39 us -> 6.24 us  [on_device(): jnp.dot(text_embeds, scaled_weight, preferred_element_type=F32)]
  transfers between devices with their start and end apart: 2 -> 2, of which waited for: 2 -> 2; matrix products, arithmetic and copies ran while one was open for 19% -> 15% of each run, Pallas kernels for 0% -> 0%
where the time goes in v3:
time: 237 us
  waiting for transfers between devices  97.4 us (41%)
  Pallas kernels  51.3 us (22%)
  matrix products  35.3 us (15%)
  other arithmetic  19.2 us (8%)
  between operations  14.3 us (6%)
  local copies, waits for them, and re-layouts  14 us (6%)
  starting transfers between devices  5.59 us (2%)
    all_gather x1, waiting for transfers between devices, on_device(): gathered = lax.all_gather(jnp.concatenate([own_grad, terms], axis=0), 'tp')  73.9 us
    pallas_call x1, Pallas kernels, reduce_all(): pl.pallas_call(functools.partial(reduce_kernel, n_grp, n_tp), out_shape=(...  51.3 us
    all_to_all x1, waiting for transfers between devices, on_device(): lax.all_to_all(image_embeds, 'tp', split_axis=1, concat_axis=0, tiled=True)  23.4 us
    dot_general x1, matrix products, on_device(): lax.dot_general(text_embeds, text_grad, over_rows, preferred_element_type...  12.6 us
    dot_general x1, matrix products, on_device(): placed = jnp.dot(place, image_keys, preferred_element_type=F32)  10.6 us
    dot_general x1, matrix products, on_device(): jnp.dot(text_embeds, scaled_weight, preferred_element_type=F32)  6.24 us
    dot_general x1, matrix products, on_device(): lax.dot_general(image_rows, image_grad, over_rows, preferred_element_type...  5.88 us
    all_to_all x1, starting transfers between devices, on_device(): lax.all_to_all(image_embeds, 'tp', split_axis=1, concat_axis=0, tiled=True)  5.55 us
  transfers between devices with their start and end apart: 2, of which 2 were waited for; matrix products, arithmetic and copies ran while one was open for 15% of the time, Pallas kernels for 0%

profile of v3, /device:TPU:1, one launch (start us, length us, event | category | flops | bytes accessed | tf_op | source)
XLA Modules:
  0.0 237.0 jit_solution(17890398638058606110)
XLA Ops:
  7.2 3.1 %multiply_reduce_fusion.1 = f32[256]{0:T(256)S(1)} fusion(bf16[256,8192]{1,0:T(8,128)(2,1)} %param.10), kind=kLoop, calls=%fused_computation.3 | loop fusion | flops 6291200 | bytes 4195328 | tf_op jit(solution)/shard_map/reduce_sum | solution.py:193
  10.4 5.1 %multiply_reduce_fusion = f32[2048]{0:T(1024)S(1)} fusion(bf16[2048,2048]{1,0:T(8,128)(2,1)} %param.9), kind=kLoop, calls=%fused_computation.1 | loop fusion | flops 12580864 | bytes 8396800 | tf_op jit(solution)/shard_map/reduce_sum | solution.py:193
  15.6 0.1 fusion.26
  15.7 0.2 multiply_convert_fusion.6
  15.9 0.8 pad_maximum_fusion
  16.8 4.7 %copy.64 = bf16[32,4,8,2048]{3,2,0,1:T(8,128)(2,1)} copy(bf16[32,4,8,2048]{3,2,1,0:T(8,128)(2,1)} %bitcast.108) | data formatting | bytes 8388608 | tf_op jit(solution)/shard_map/all_to_all | solution.py:210
  21.5 5.6 %all-to-all-start = ((bf16[256,4,2048]{2,0,1:T(8,128)(2,1)}), bf16[256,4,2048]{2,0,1:T(8,128)(2,1)}, u32[]{:S(2)}, u32[]{:S(2)}) async-start(bf16[256,4,2048]{2,0,1:T(8,128)(2,1)} %bitcast.109), calls=%async_computation | async-start | bytes 8388608 | tf_op jit(solution)/shard_map/all_to_all | solution.py:210
  27.2 0.1 add.81
  27.2 0.1 fusion.27
  27.4 0.2 slice_reduce_fusion.1
  27.6 0.1 and.57
  27.7 0.1 and.52
  27.8 0.1 reshape.210
  28.0 0.2 slice_reduce_fusion.3
  28.2 0.1 broadcast_bitcast_fusion
  28.4 2.4 %fusion = bf16[2048,1024]{1,0:T(8,128)(2,1)} fusion(s32[2048]{0:T(1024)S(1)} %get-tuple-element.26), kind=kLoop, calls=%fused_computation.4 | loop fusion | flops 4194304 | bytes 4202496 | tf_op jit(solution)/shard_map/convert_element_type | solution.py:247
  30.9 73.9 %all-gather.3.cloned.1.call-done = bf16[2112,512]{1,0:T(8,128)(2,1)} async-done(((bf16[528,512]{1,0:T(8,128)(2,1)}), bf16[2112,512]{1,0:T(8,128)(2,1)}) %all-gather.3.cloned.1.call-update) | async-done | bytes 2162704 | tf_op jit(solution)/shard_map/all_gather | solution.py:203
  104.8 1.7 slice.51
  106.6 0.8 slice_bitcast_fusion
  107.6 4.0 %gather_fusion = bf16[1024,512]{1,0:T(8,128)(2,1)S(1)} fusion(bf16[2048,512]{1,0:T(8,128)(2,1)S(1)} %bitcast.105, s32[1024]{0:T(1024)S(1)} %broadcast_clamp_fusion), kind=kCustom, calls=%fused_computation | custom fusion | bytes 2101248 | tf_op jit(solution)/shard_map/jit(_take)/gather | solution.py:239
  111.6 0.3 convert_reduce_fusion.bias_ref
  111.9 1.3 multiply_convert_fusion.4
  113.2 12.6 %convolution_bitcast_fusion = f32[2048,512]{1,0:T(8,128)} fusion(bf16[2048,2048]{1,0:T(8,128)(2,1)} %param.9, bf16[2048,512]{1,0:T(8,128)(2,1)S(1)} %bitcast.107, f32[2048]{0:T(1024)S(1)} %slice_multiply_fusion), kind=kOutput, calls=%fused_computation.16 | convolution fusion | flops 4298113024 | bytes 14688256 | tf_op jit(solution)/shard_map/dot_general | solution.py:242
  125.9 6.2 %fusion.3 = bf16[2048,512]{1,0:T(8,128)(2,1)} fusion(bf16[2048,2048]{1,0:T(8,128)(2,1)S(1)} %bitcast.111, f32[2048]{0:T(1024)S(1)} %slice_multiply_fusion, bf16[2048,512]{1,0:T(8,128)(2,1)S(1)} %copy-done.2, f32[2048]{0:T(1024)S(1)} %convert_element_type.90), kind=kOutput, calls=%fused_computation.17 | convolution fusion | flops 4300210176 | bytes 12599296 | tf_op jit(solution)/shard_map/dot_general | solution.py:230
  132.1 23.4 %all-to-all-done = bf16[256,4,2048]{2,0,1:T(8,128)(2,1)} async-done(((bf16[256,4,2048]{2,0,1:T(8,128)(2,1)}), bf16[256,4,2048]{2,0,1:T(8,128)(2,1)}, u32[]{:S(2)}, u32[]{:S(2)}) %all-to-all-start) | async-done | bytes 4194336 | tf_op jit(solution)/shard_map/all_to_all | solution.py:210
  155.5 5.9 %add_convert_fusion.weight_ref = bf16[2048,512]{1,0:T(8,128)(2,1)S(1)} fusion(f32[2048,512]{1,0:T(8,128)} %convolution_bitcast_fusion, bf16[1024,2048]{1,0:T(8,128)(2,1)} %bitcast.1, bf16[1024,512]{1,0:T(8,128)(2,1)S(1)} %copy-done.4), kind=kOutput, calls=%fused_computation.12 | convolution fusion | flops 2149580800 | bytes 11534336 | tf_op jit(solution)/shard_map/dot_general | solution.py:256
  161.4 10.6 %add_convert_fusion.1.keys_ref = bf16[2048,512]{1,0:T(8,128)(2,1)} fusion(bf16[2048,512]{1,0:T(8,128)(2,1)} %fusion.3, bf16[2048,1024]{1,0:T(8,128)(2,1)} %fusion, bf16[1024,2048]{1,0:T(8,128)(2,1)} %bitcast.1, f32[1024]{0:T(1024)S(1)} %get-tuple-element.31, bf16[2048,512]{1,0:T(8,128)(2,1)} %param.15, f32[2048]{0:T(1024)S(1)} %convert_element_type.90), kind=kOutput, calls=%fused_computation.13 | convolution fusion | flops 4302307328 | bytes 14692352 | tf_op jit(solution)/shard_map/dot_general | solution.py:254
  172.0 1.6 copy-done.1
  173.6 51.3 %shard_map.120 = (f32[512,512]{1,0:T(8,128)S(1)}, bf16[2048,512]{1,0:T(8,128)(2,1)S(1)}, f32[8,512]{1,0:T(8,128)S(1)}) custom-call(bf16[2048,512]{1,0:T(8,128)(2,1)S(1)} %copy-done.1, bf16[2048,512]{1,0:T(8,128)(2,1)S(1)} %add_convert_fusion.weight_ref, f32[8,512]{1,0:T(8,128)S(1)} %convert_reduce_fusion.bias_ref), custom_call_target="tpu_custom_call" | custom-call | tf_op jit(solution)/shard_map/pallas_call | solution.py:131
  224.9 3.7 %fusion.2 = (f32[2048]{0:T(1024)}, f32[2048,512]{1,0:T(8,128)}) fusion(bf16[2048,512]{1,0:T(8,128)(2,1)S(1)} %copy-done.3, bf16[2048,512]{1,0:T(8,128)(2,1)S(1)} %get-tuple-element.18, f32[2048]{0:T(1024)S(1)} %convert_element_type.90), kind=kLoop, calls=%fused_computation.9 | loop fusion | flops 5240832 | bytes 8404992 | tf_op jit(solution)/shard_map/reduce_sum | solution.py:272
  228.6 0.9 multiply_convert_fusion.5
  229.5 0.6 reduce_sum.68
  (57 shorter events, 0.8 us)
Async XLA Ops:
  7.2 8.4 %copy-start = (s32[2]{0:T(128)S(1)}, s32[2]{0:T(128)}, u32[]{:S(2)}) copy-start(s32[2]{0:T(128)} %param.13) | copy-start | bytes 28
  7.2 97.6 %all-gather.3.cloned.1.call-start = ((), (), s32[]{:S(2)}) async-start(), calls=%async_computation.1 | async-start | bytes 2703360 | tf_op jit(solution)/shard_map/all_gather | solution.py:203
  10.3 5.4 %copy-start.5 = (bf16[512,512]{1,0:T(8,128)(2,1)S(1)}, bf16[512,512]{1,0:T(8,128)(2,1)}, u32[]{:S(2)}) copy-start(bf16[512,512]{1,0:T(8,128)(2,1)} %param.17) | copy-start | bytes 1572868
  21.5 5.6 %copy-start.6 = (s32[2,2]{1,0:T(2,128)S(1)}, s32[2,2]{1,0:T(2,128)}, u32[]{:S(2)}) copy-start(s32[2,2]{1,0:T(2,128)} %param.11) | copy-start | bytes 52
  21.5 5.7 %copy-start.9 = (s32[2]{0:T(128)S(1)}, s32[2]{0:T(128)}, u32[]{:S(2)}) copy-start(s32[2]{0:T(128)} %param.12) | copy-start | bytes 28
  21.5 6.3 %copy-start.7 = (bf16[2048]{0:T(1024)(128)(2,1)S(1)}, bf16[2048]{0:T(1024)(128)(2,1)}, u32[]{:S(2)}) copy-start(bf16[2048]{0:T(1024)(128)(2,1)} %param.14) | copy-start | bytes 12292
  21.5 6.4 %copy-start.8 = (bf16[512]{0:T(512)(128)(2,1)S(1)}, bf16[512]{0:T(512)(128)(2,1)}, u32[]{:S(2)}) copy-start(bf16[512]{0:T(512)(128)(2,1)} %param.16) | copy-start | bytes 3076
  21.5 134.0 %all-to-all-start = ((bf16[256,4,2048]{2,0,1:T(8,128)(2,1)}), bf16[256,4,2048]{2,0,1:T(8,128)(2,1)}, u32[]{:S(2)}, u32[]{:S(2)}) async-start(bf16[256,4,2048]{2,0,1:T(8,128)(2,1)} %bitcast.109), calls=%async_computation | async-start | bytes 8388608 | tf_op jit(solution)/shard_map/all_to_all | solution.py:210
  111.9 13.9 %slice-start = ((s8[8388608]{0:T(1024)(128)(4,1)}), s8[4194304]{0:T(1024)(128)(4,1)S(1)}, s32[]{:S(2)}) async-start(s8[8388608]{0:T(1024)(128)(4,1)} %bitcast.110), calls=%async_computation.2 | async-start | bytes 8388608
  113.2 12.6 %slice-start.1 = ((s8[8388608]{0:T(1024)(128)(4,1)}), s8[4194304]{0:T(1024)(128)(4,1)S(1)}, s32[]{:S(2)}) async-start(s8[8388608]{0:T(1024)(128)(4,1)} %bitcast.110), calls=%async_computation.3 | async-start | bytes 8388608
  113.2 12.6 %copy-start.2 = (bf16[2048,512]{1,0:T(8,128)(2,1)S(1)}, bf16[2048,512]{1,0:T(8,128)(2,1)}, u32[]{:S(2)}) copy-start(bf16[2048,512]{1,0:T(8,128)(2,1)} %param.15) | copy-start | bytes 6291460
  125.8 29.7 %copy-start.4 = (bf16[1024,512]{1,0:T(8,128)(2,1)S(1)}, bf16[1024,512]{1,0:T(8,128)(2,1)}, u32[]{:S(2)}) copy-start(bf16[1024,512]{1,0:T(8,128)(2,1)} %multiply_convert_fusion.4) | copy-start | bytes 3145732
  172.0 1.6 copy-start.1
  173.6 51.3 %copy-start.3 = (bf16[2048,512]{1,0:T(8,128)(2,1)S(1)}, bf16[2048,512]{1,0:T(8,128)(2,1)}, u32[]{:S(2)}) copy-start(bf16[2048,512]{1,0:T(8,128)(2,1)} %param.15) | copy-start | bytes 6291460
Sparse Core Ops, SparseCore 0:
  16.9 87.8 all-gather.2

commit v4 on v3

--- a/solution.py
+++ b/solution.py
@@ -158,6 +158,91 @@
     )(keys, weight, bias)
 
 
+def relay_kernel(
+    n_tp, pieces, own_ref, out_ref, held, right_send, right_recv, left_send, left_recv
+):
+    t = lax.axis_index("tp")
+    size = own_ref.shape[0] // pieces
+    last = n_tp - 1
+
+    barrier = pltpu.get_barrier_semaphore()
+
+    for d in range(1, n_tp):
+        pl.semaphore_signal(barrier, inc=1, device_id={"tp": lax.rem(t + d, n_tp)})
+    pl.semaphore_wait(barrier, n_tp - 1)
+
+    def move(step, piece, to_right):
+        rows = pl.ds(piece * size, size)
+        block = t - step if to_right else t + step
+        block = jnp.clip(block, 0, last)
+        source = own_ref.at[rows] if step == 0 else held.at[block, rows]
+        send, recv = (right_send, right_recv) if to_right else (left_send, left_recv)
+        peer = jnp.minimum(t + 1, last) if to_right else jnp.maximum(t - 1, 0)
+        return pltpu.make_async_remote_copy(
+            src_ref=source,
+            dst_ref=held.at[block, rows],
+            send_sem=send.at[step, piece],
+            recv_sem=recv.at[step, piece],
+            device_id={"tp": peer},
+        )
+
+    def sends(step, to_right):
+        if to_right:
+            return (t < last) & (t >= step)
+        return (t > 0) & (t + step <= last)
+
+    def receives(step, to_right):
+        return t >= step + 1 if to_right else t + step + 1 <= last
+
+    for step in range(n_tp - 1):
+        for piece in range(pieces):
+            for to_right in (True, False):
+                if step > 0:
+
+                    @pl.when(receives(step - 1, to_right))
+                    def _():
+                        move(step - 1, piece, to_right).wait_recv()
+
+                @pl.when(sends(step, to_right))
+                def _():
+                    move(step, piece, to_right).start()
+
+    for piece in range(pieces):
+        for to_right in (True, False):
+
+            @pl.when(receives(n_tp - 2, to_right))
+            def _():
+                move(n_tp - 2, piece, to_right).wait_recv()
+
+    for step in range(n_tp - 1):
+        for piece in range(pieces):
+            for to_right in (True, False):
+
+                @pl.when(sends(step, to_right))
+                def _():
+                    move(step, piece, to_right).wait_send()
+
+    held[t] = own_ref[...]
+    out_ref[...] = held[...]
+
+
+def relay_gather(n_tp, own):
+    pieces = 3 if own.shape[0] % 48 == 0 else 1
+    vmem = pl.BlockSpec(memory_space=pltpu.VMEM)
+    full = (n_tp,) + own.shape
+    return pl.pallas_call(
+        functools.partial(relay_kernel, n_tp, pieces),
+        out_shape=jax.ShapeDtypeStruct(full, own.dtype),
+        in_specs=[vmem],
+        out_specs=vmem,
+        scratch_shapes=[pltpu.VMEM(full, own.dtype)]
+        + [pltpu.SemaphoreType.DMA((n_tp - 1, pieces))] * 4,
+        compiler_params=pltpu.CompilerParams(
+            collective_id=1, has_side_effects=True, vmem_limit_bytes=16 * 1024 * 1024
+        ),
+    )(own)
+
+
 def on_device(
     text_embeds,
     image_embeds,
@@ -200,7 +285,8 @@
     count = own_squares.shape[0]
     extra = -(-3 * count // (16 * columns)) * 16
     terms = jnp.pad(terms, (0, extra * columns - 3 * count)).reshape(extra, columns)
-    gathered = lax.all_gather(jnp.concatenate([own_grad, terms], axis=0), "tp")
+    gathered = relay_gather(n_tp, jnp.concatenate([own_grad, terms], axis=0))
+    gathered, image_embeds = lax.optimization_barrier((gathered, image_embeds))
     masked_grad = gathered[:, :own_count].reshape(rows, columns)
     terms = gathered[:, own_count:].reshape(n_tp, extra * columns)[:, : 3 * count]
     parts = jnp.sum(terms.astype(F32).reshape(n_tp, 3, count), axis=1)

time: 237 us -> 225 us (0.949)
  Pallas kernels: 51.3 us -> 92.1 us
  waiting for transfers between devices: 97.4 us -> 60.7 us
  between operations: 14.3 us -> 0.96 us
    all_gather x1 -> x0, waiting for transfers between devices: 73.9 us -> none  [on_device(): gathered = lax.all_gather(jnp.concatenate([own_grad, terms], axis=0), 'tp')]
    pallas_call x0 -> x1, Pallas kernels: none -> 39.8 us  [relay_gather(): pl.pallas_call(functools.partial(relay_kernel, n_tp, pieces), out_shape=j...]
    all_to_all x1, waiting for transfers between devices: 23.4 us -> 60.7 us  [on_device(): lax.all_to_all(image_embeds, 'tp', split_axis=1, concat_axis=0, tiled=True)]
    all_to_all x1, local copies, waits for them, and re-layouts: 4.75 us -> 2.28 us  [on_device(): lax.all_to_all(image_embeds, 'tp', split_axis=1, concat_axis=0, tiled=True)]
  transfers between devices with their start and end apart: 2 -> 1, of which waited for: 2 -> 1; matrix products, arithmetic and copies ran while one was open for 15% -> 14% of each run, Pallas kernels for 0% -> 0%
where the time goes in v4:
time: 225 us
  Pallas kernels  92.1 us (41%)
  waiting for transfers between devices  60.7 us (27%)
  matrix products  34.9 us (16%)
  other arithmetic  18.5 us (8%)
  local copies, waits for them, and re-layouts  12.5 us (6%)
  starting transfers between devices  5.04 us (2%)
    all_to_all x1, waiting for transfers between devices, on_device(): lax.all_to_all(image_embeds, 'tp', split_axis=1, concat_axis=0, tiled=True)  60.7 us
    pallas_call x1, Pallas kernels, reduce_all(): pl.pallas_call(functools.partial(reduce_kernel, n_grp, n_tp), out_shape=(...  52.2 us
    pallas_call x1, Pallas kernels, relay_gather(): pl.pallas_call(functools.partial(relay_kernel, n_tp, pieces), out_shape=j...  39.8 us
    dot_general x1, matrix products, on_device(): lax.dot_general(text_embeds, text_grad, over_rows, preferred_element_type...  12.5 us
    dot_general x1, matrix products, on_device(): placed = jnp.dot(place, image_keys, preferred_element_type=F32)  10.6 us
    gather x1, local copies, waits for them, and re-layouts, on_device(): picked = jnp.take(masked_grad, image_at, axis=0, mode='clip')  6 us
    dot_general x1, matrix products, on_device(): jnp.dot(text_embeds, scaled_weight, preferred_element_type=F32)  5.99 us
    dot_general x1, matrix products, on_device(): lax.dot_general(image_rows, image_grad, over_rows, preferred_element_type...  5.88 us
  transfers between devices with their start and end apart: 1, of which 1 were waited for; matrix products, arithmetic and copies ran while one was open for 14% of the time, Pallas kernels for 0%

profile of v4, /device:TPU:1, one launch (start us, length us, event | category | flops | bytes accessed | tf_op | source)
XLA Modules:
  0.0 224.7 jit_solution(8736835620047587696)
XLA Ops:
  0.7 3.1 %multiply_reduce_fusion.1 = f32[256]{0:T(256)S(1)} fusion(bf16[256,8192]{1,0:T(8,128)(2,1)} %param.10), kind=kLoop, calls=%fused_computation.3 | loop fusion | flops 6291200 | bytes 4195328 | tf_op jit(solution)/shard_map/reduce_sum | solution.py:278
  3.8 5.1 %multiply_reduce_fusion = f32[2048]{0:T(1024)S(1)} fusion(bf16[2048,2048]{1,0:T(8,128)(2,1)} %param.9), kind=kLoop, calls=%fused_computation.1 | loop fusion | flops 12580864 | bytes 8396800 | tf_op jit(solution)/shard_map/reduce_sum | solution.py:278
  9.1 0.1 fusion.26
  9.1 0.2 multiply_convert_fusion.6
  9.4 39.8 %shard_map.120 = bf16[4,528,512]{2,1,0:T(8,128)(2,1)S(1)} custom-call(bf16[528,512]{1,0:T(8,128)(2,1)S(1)} %pad_maximum_fusion.own_ref), custom_call_target="tpu_custom_call" | custom-call | tf_op jit(solution)/shard_map/pallas_call | solution.py:233
  49.2 2.3 %copy.64 = bf16[32,4,8,2048]{3,2,0,1:T(8,128)(2,1)} copy(bf16[32,4,8,2048]{3,2,1,0:T(8,128)(2,1)S(1)} %bitcast.107) | data formatting | bytes 8388608 | tf_op jit(solution)/shard_map/all_to_all | solution.py:296
  51.5 5.0 %all-to-all-start = ((bf16[256,4,2048]{2,0,1:T(8,128)(2,1)}), bf16[256,4,2048]{2,0,1:T(8,128)(2,1)}, u32[]{:S(2)}, u32[]{:S(2)}) async-start(bf16[256,4,2048]{2,0,1:T(8,128)(2,1)} %bitcast.108), calls=%async_computation | async-start | bytes 8388608 | tf_op jit(solution)/shard_map/all_to_all | solution.py:296
  56.6 1.5 slice.42
  58.3 0.1 fusion.27
  58.3 0.2 slice_reduce_fusion.1
  58.5 0.1 and.57
  58.6 0.1 and.52
  58.8 0.1 add.81
  58.9 0.1 add_bitcast_fusion
  59.0 0.1 reshape.210
  59.1 0.1 broadcast_bitcast_fusion.7
  59.2 6.0 %gather_fusion = bf16[1024,512]{1,0:T(8,128)(2,1)S(1)} fusion(bf16[2048,512]{1,0:T(8,128)(2,1)} %bitcast.104, s32[1024]{0:T(1024)S(1)} %broadcast_clamp_fusion), kind=kCustom, calls=%fused_computation | custom fusion | bytes 2101248 | tf_op jit(solution)/shard_map/jit(_take)/gather | solution.py:325
  65.2 0.2 slice_reduce_fusion.3
  65.5 0.3 convert_reduce_fusion.bias_ref
  65.8 0.1 broadcast_bitcast_fusion
  66.1 1.3 multiply_convert_fusion.4
  67.4 2.5 %fusion = bf16[2048,1024]{1,0:T(8,128)(2,1)} fusion(s32[2048]{0:T(1024)S(1)} %get-tuple-element.30), kind=kLoop, calls=%fused_computation.4 | loop fusion | flops 4194304 | bytes 4202496 | tf_op jit(solution)/shard_map/convert_element_type | solution.py:333
  69.9 12.5 %convolution_bitcast_fusion = f32[2048,512]{1,0:T(8,128)} fusion(bf16[2048,2048]{1,0:T(8,128)(2,1)} %param.9, bf16[2048,512]{1,0:T(8,128)(2,1)S(1)} %bitcast.106, f32[2048]{0:T(1024)S(1)} %slice_multiply_fusion), kind=kOutput, calls=%fused_computation.16 | convolution fusion | flops 4298113024 | bytes 14688256 | tf_op jit(solution)/shard_map/dot_general | solution.py:328
  82.4 6.0 %fusion.3 = bf16[2048,512]{1,0:T(8,128)(2,1)} fusion(bf16[2048,2048]{1,0:T(8,128)(2,1)S(1)} %bitcast.110, f32[2048]{0:T(1024)S(1)} %slice_multiply_fusion, bf16[2048,512]{1,0:T(8,128)(2,1)S(1)} %copy-done.4, f32[2048]{0:T(1024)S(1)} %convert_element_type.95), kind=kOutput, calls=%fused_computation.17 | convolution fusion | flops 4300210176 | bytes 12599296 | tf_op jit(solution)/shard_map/dot_general | solution.py:316
  88.4 60.7 %all-to-all-done = bf16[256,4,2048]{2,0,1:T(8,128)(2,1)} async-done(((bf16[256,4,2048]{2,0,1:T(8,128)(2,1)}), bf16[256,4,2048]{2,0,1:T(8,128)(2,1)}, u32[]{:S(2)}, u32[]{:S(2)}) %all-to-all-start) | async-done | bytes 4194336 | tf_op jit(solution)/shard_map/all_to_all | solution.py:296
  149.1 5.9 %add_convert_fusion.weight_ref = bf16[2048,512]{1,0:T(8,128)(2,1)S(1)} fusion(f32[2048,512]{1,0:T(8,128)} %convolution_bitcast_fusion, bf16[1024,2048]{1,0:T(8,128)(2,1)} %bitcast.1, bf16[1024,512]{1,0:T(8,128)(2,1)S(1)} %copy-done.6), kind=kOutput, calls=%fused_computation.12 | convolution fusion | flops 2149580800 | bytes 11534336 | tf_op jit(solution)/shard_map/dot_general | solution.py:342
  155.0 10.6 %add_convert_fusion.1.keys_ref = bf16[2048,512]{1,0:T(8,128)(2,1)} fusion(bf16[2048,512]{1,0:T(8,128)(2,1)} %fusion.3, bf16[2048,1024]{1,0:T(8,128)(2,1)} %fusion, bf16[1024,2048]{1,0:T(8,128)(2,1)} %bitcast.1, f32[1024]{0:T(1024)S(1)} %get-tuple-element.35, bf16[2048,512]{1,0:T(8,128)(2,1)} %param.15, f32[2048]{0:T(1024)S(1)} %convert_element_type.95), kind=kOutput, calls=%fused_computation.13 | convolution fusion | flops 4302307328 | bytes 14692352 | tf_op jit(solution)/shard_map/dot_general | solution.py:340
  165.6 1.6 copy-done.1
  167.2 52.2 %shard_map.121 = (f32[512,512]{1,0:T(8,128)S(1)}, bf16[2048,512]{1,0:T(8,128)(2,1)S(1)}, f32[8,512]{1,0:T(8,128)S(1)}) custom-call(bf16[2048,512]{1,0:T(8,128)(2,1)S(1)} %copy-done.1, bf16[2048,512]{1,0:T(8,128)(2,1)S(1)} %add_convert_fusion.weight_ref, f32[8,512]{1,0:T(8,128)S(1)} %convert_reduce_fusion.bias_ref), custom_call_target="tpu_custom_call" | custom-call | tf_op jit(solution)/shard_map/pallas_call | solution.py:131
  219.5 3.7 %fusion.2 = (f32[2048]{0:T(1024)}, f32[2048,512]{1,0:T(8,128)}) fusion(bf16[2048,512]{1,0:T(8,128)(2,1)S(1)} %copy-done.5, bf16[2048,512]{1,0:T(8,128)(2,1)S(1)} %get-tuple-element.22, f32[2048]{0:T(1024)S(1)} %convert_element_type.95), kind=kLoop, calls=%fused_computation.9 | loop fusion | flops 5240832 | bytes 8404992 | tf_op jit(solution)/shard_map/reduce_sum | solution.py:358
  223.2 1.0 multiply_convert_fusion.5
  224.1 0.6 reduce_sum.68
  (59 shorter events, 0.7 us)
Async XLA Ops:
  0.6 8.3 %copy-start = (s32[2]{0:T(128)S(1)}, s32[2]{0:T(128)}, u32[]{:S(2)}) copy-start(s32[2]{0:T(128)} %param.13) | copy-start | bytes 28
  3.8 5.4 %copy-start.7 = (bf16[512,512]{1,0:T(8,128)(2,1)S(1)}, bf16[512,512]{1,0:T(8,128)(2,1)}, u32[]{:S(2)}) copy-start(bf16[512,512]{1,0:T(8,128)(2,1)} %param.17) | copy-start | bytes 1572868
  9.1 40.1 %copy-start.3 = (bf16[256,8192]{1,0:T(8,128)(2,1)S(1)}, bf16[256,8192]{1,0:T(8,128)(2,1)}, u32[]{:S(2)}) copy-start(bf16[256,8192]{1,0:T(8,128)(2,1)} %param.10) | copy-start | bytes 12582916
  51.5 97.6 %all-to-all-start = ((bf16[256,4,2048]{2,0,1:T(8,128)(2,1)}), bf16[256,4,2048]{2,0,1:T(8,128)(2,1)}, u32[]{:S(2)}, u32[]{:S(2)}) async-start(bf16[256,4,2048]{2,0,1:T(8,128)(2,1)} %bitcast.108), calls=%async_computation | async-start | bytes 8388608 | tf_op jit(solution)/shard_map/all_to_all | solution.py:296
  56.5 1.7 copy-start.11
  56.6 2.2 copy-start.9
  56.6 2.2 copy-start.8
  56.6 2.6 %copy-start.10 = (bf16[512]{0:T(512)(128)(2,1)S(1)}, bf16[512]{0:T(512)(128)(2,1)}, u32[]{:S(2)}) copy-start(bf16[512]{0:T(512)(128)(2,1)} %param.16) | copy-start | bytes 3076
  59.2 6.3 %copy-start.2 = (bf16[4,512,512]{2,1,0:T(8,128)(2,1)S(1)}, bf16[4,512,512]{2,1,0:T(8,128)(2,1)}, u32[]{:S(2)}) copy-start(bf16[4,512,512]{2,1,0:T(8,128)(2,1)} %slice.42) | copy-start | bytes 6291460
  67.4 15.0 %slice-start = ((s8[8388608]{0:T(1024)(128)(4,1)}), s8[4194304]{0:T(1024)(128)(4,1)S(1)}, s32[]{:S(2)}) async-start(s8[8388608]{0:T(1024)(128)(4,1)} %bitcast.109), calls=%async_computation.1 | async-start | bytes 8388608
  69.9 12.5 %slice-start.1 = ((s8[8388608]{0:T(1024)(128)(4,1)}), s8[4194304]{0:T(1024)(128)(4,1)S(1)}, s32[]{:S(2)}) async-start(s8[8388608]{0:T(1024)(128)(4,1)} %bitcast.109), calls=%async_computation.2 | async-start | bytes 8388608
  69.9 12.5 %copy-start.4 = (bf16[2048,512]{1,0:T(8,128)(2,1)S(1)}, bf16[2048,512]{1,0:T(8,128)(2,1)}, u32[]{:S(2)}) copy-start(bf16[2048,512]{1,0:T(8,128)(2,1)} %param.15) | copy-start | bytes 6291460
  82.4 66.7 %copy-start.6 = (bf16[1024,512]{1,0:T(8,128)(2,1)S(1)}, bf16[1024,512]{1,0:T(8,128)(2,1)}, u32[]{:S(2)}) copy-start(bf16[1024,512]{1,0:T(8,128)(2,1)} %multiply_convert_fusion.4) | copy-start | bytes 3145732
  165.6 1.6 copy-start.1
  167.2 52.2 %copy-start.5 = (bf16[2048,512]{1,0:T(8,128)(2,1)S(1)}, bf16[2048,512]{1,0:T(8,128)(2,1)}, u32[]{:S(2)}) copy-start(bf16[2048,512]{1,0:T(8,128)(2,1)} %param.15) | copy-start | bytes 6291460
